TPU v7x, 512 devices: a whole 4x4x16 slice. The times are simulated.
512 devices in a mesh: dp: 16 (over x_lo, y, core), ctx: 32 (over z, x_hi).
Axes of the slice: x: 4 (x_hi: 2, x_lo: 2; x = x_hi * 2 + x_lo), y: 4, z: 16, core: 2. Of those that a mesh axis runs over, the one named last changes fastest.
Arguments:
- span_ids: int32 [16, 64], P('dp'), may hold values from 0 to 63, as said below
- hidden_in: bfloat16 [16, 4096, 4096], P('dp', 'ctx'), may hold values from -6 to 6
- queries: bfloat16 [16, 4096, 2048], P('dp', 'ctx'), may hold values from -64 to 64
- keys_in: bfloat16 [16, 4096, 512], P('dp', 'ctx'), may hold values from -4 to 4
- values_in: bfloat16 [16, 4096, 512], P('dp', 'ctx'), may hold values from -4 to 4
- attn_out: bfloat16 [16, 4096, 2048], P('dp', 'ctx'), may hold values from -4 to 4, as said below
- out_grad: bfloat16 [16, 4096, 2048], P('dp', 'ctx'), may hold values from -6 to 6
- log_norm: float32 [16, 4096, 16], P('dp', 'ctx'), may hold values from -300 to 3000, as said below
- adapter: float32 [8, 5120], P(None, 'dp'), may hold values from -0.3 to 0.3
- moment_first: float32 [8, 5120], P(None, 'dp'), may hold values from -0.0078125 to 0.0078125
- moment_second: float32 [8, 5120], P(None, 'dp'), may hold values from 6.103516e-08 to 9.765625e-07
Outputs:
- query_grad: bfloat16 [16, 4096, 2048], P('dp', 'ctx')
- kv_grad: bfloat16 [16, 4096, 1024], P('dp', 'ctx')
- adapter_step: float32 [8, 5120], P(None, 'dp')
Inputs may be any that keep to these rules, and one draw needn't show every extreme that they name: `span_ids`: in each sequence the entries 2c and 2c + 1 belong to device c of ctx; entry 2c + 1 equals 63 minus entry 2c, and the entries 2c over all c are a permutation of 0 to 31, drawn afresh for every sequence. `attn_out`: the saved softmax output of queries, keys_in and values_in under the causal mask by pos. `log_norm`: the log of the causal softmax total of each query row and head.
All inputs are finite; a program needn't handle non-finite values.
Results may differ from a plain program's by a relative error of at most 0.017.
Values may be sent and summed in bfloat16 or wider, within the bound.
No kernel may reach another device: no remote copies, remote signals or barrier semaphores. Data moves between devices by JAX's collectives and lax.ppermute only.
A program may use at most 128 MiB of HBM per device.

v0:
```python
import jax
import jax.numpy as jnp
from jax import lax
from jax.sharding import Mesh
from jax.sharding import PartitionSpec as P

D = 4096
H = 16
KVH = 4
DH = 128
ROWS = 128
HALF = 64
CTX = ("ctx_0", "ctx_1")


BIAS_ONE = 1.0 - 0.9**100.0
BIAS_TWO = 1.0 - 0.999**100.0


def in_one_piece(arrays, axis, dim, along):
    both = jnp.concatenate(arrays, axis=along)
    filled, at, finished = (lax.all_gather(both, axis, axis=dim, tiled=True), 0, [])
    for a in arrays:
        finished.append(lax.slice_in_dim(filled, at, at + a.shape[along], axis=along))
        at += a.shape[along]
    return tuple(finished)


def summed_rows(shard, axes, dim):
    if not axes:
        return shard
    nearer = lax.psum_scatter(shard, axes[0], scatter_dimension=dim, tiled=True)
    return summed_rows(nearer, axes[1:], dim)


def in_order(pieces, dim):
    dims = list(pieces.shape[1:])
    dims[dim] *= pieces.shape[0]
    return jnp.moveaxis(pieces, 0, dim).reshape(dims)


def from_everyone(shard, axis):
    count = lax.axis_size(axis)
    return lax.all_to_all(
        jnp.broadcast_to(shard[None], (count, *shard.shape)), axis, 0, 0, tiled=True
    )


def gathered_copies(shard, axis, dim):
    return in_order(from_everyone(shard, axis), dim)


def cut_along(shard, dim, count):
    dims = shard.shape
    pieces = shard.reshape(*dims[:dim], count, dims[dim] // count, *dims[dim + 1 :])
    return jnp.moveaxis(pieces, dim, 0)


def summed_on_arrival(shard, axis, dim):
    pieces = cut_along(shard, dim, lax.axis_size(axis))
    arrived = lax.all_to_all(pieces, axis, split_axis=0, concat_axis=0, tiled=True)
    return arrived.astype(jnp.float32).sum(axis=0)


def of_everyone(shard, axis):
    return from_everyone(shard, axis).sum(axis=0)


def grouped(rows):
    return rows.reshape(rows.shape[0], KVH, H // KVH, DH)


def per_head(stat_rows):
    return jnp.transpose(stat_rows.reshape(stat_rows.shape[0], KVH, H // KVH), (1, 2, 0))[..., None]


def block_terms(
    query_rows, grad_rows, norm_rows, delta_rows, pos_query, key_rows, value_rows, pos_keys
):
    score_scale = DH ** (-0.5)
    scores = (
        jnp.einsum("rkgd,skd->kgrs", query_rows, key_rows, preferred_element_type=jnp.float32)
        * score_scale
    )
    visible = pos_keys[None, :] <= pos_query[:, None]
    weights = jnp.where(visible, jnp.exp(scores - norm_rows), 0.0)
    weights_low = weights.astype(jnp.bfloat16)
    d_weights = jnp.einsum(
        "rkgd,skd->kgrs", grad_rows, value_rows, preferred_element_type=jnp.float32
    )
    d_scores = (weights * (d_weights - delta_rows)).astype(jnp.bfloat16)
    query_part = (
        jnp.einsum("kgrs,skd->rkgd", d_scores, key_rows, preferred_element_type=jnp.float32)
        * score_scale
    )
    key_part = (
        jnp.einsum("kgrs,rkgd->skd", d_scores, query_rows, preferred_element_type=jnp.float32)
        * score_scale
    )
    value_part = jnp.einsum(
        "kgrs,rkgd->skd", weights_low, grad_rows, preferred_element_type=jnp.float32
    )
    key_count = key_rows.shape[0]
    kv_part = jnp.concatenate(
        [key_part.reshape(key_count, KVH * DH), value_part.reshape(key_count, KVH * DH)], axis=1
    )
    return (query_part, kv_part)


def per_device(
    span_ids,
    hidden_in,
    queries,
    keys_in,
    values_in,
    attn_out,
    out_grad,
    log_norm,
    adapter,
    moment_first,
    moment_second,
):
    assignment = span_ids[0]
    span_count = assignment.shape[0]
    length_all = span_count * HALF
    kv_width = 2 * KVH * DH
    me_ctx = lax.axis_index(CTX)
    own_spans = lax.dynamic_slice_in_dim(assignment, 2 * me_ctx, 2)
    query_rows = grouped(queries[0])
    grad_rows = grouped(out_grad[0])
    norm_rows = per_head(log_norm[0])
    products = out_grad[0].astype(jnp.float32) * attn_out[0].astype(jnp.float32)
    delta_rows = per_head(jnp.sum(products.reshape(ROWS, H, DH), axis=-1))
    key_all, value_all = in_one_piece((keys_in[0], values_in[0]), CTX, 0, 1)
    span_keys = key_all.reshape(span_count, HALF, KVH, DH)
    span_values = value_all.reshape(span_count, HALF, KVH, DH)
    span_iota = jnp.arange(span_count, dtype=jnp.int32)
    slot_of = jnp.sum(
        jnp.where(assignment[None, :] == span_iota[:, None], span_iota[None, :], 0), axis=1
    )
    key_block = min(512, length_all)
    per_block = key_block // HALF
    early_span = own_spans[0]
    late_span = own_spans[1]
    early_limit = ((early_span + 1) * HALF + key_block - 1) // key_block
    late_limit = ((late_span + 1) * HALF + key_block - 1) // key_block
    early_range = slice(0, HALF)
    late_range = slice(HALF, ROWS)
    pos_early = early_span * HALF + jnp.arange(HALF, dtype=jnp.int32)
    pos_late = late_span * HALF + jnp.arange(HALF, dtype=jnp.int32)
    zero_query = jnp.zeros((HALF, KVH, H // KVH, DH), jnp.float32)

    def block_step(block_idx, totals):
        early_sum, late_sum, grad_low = totals
        slot_rows = lax.dynamic_slice_in_dim(slot_of, block_idx * per_block, per_block)
        key_rows = span_keys[slot_rows].reshape(key_block, KVH, DH)
        value_rows = span_values[slot_rows].reshape(key_block, KVH, DH)
        pos_keys = block_idx * key_block + jnp.arange(key_block, dtype=jnp.int32)
        late_query, late_kv = block_terms(
            query_rows[late_range],
            grad_rows[late_range],
            norm_rows[:, :, late_range],
            delta_rows[:, :, late_range],
            pos_late,
            key_rows,
            value_rows,
            pos_keys,
        )

        def with_early(unused):
            return block_terms(
                query_rows[early_range],
                grad_rows[early_range],
                norm_rows[:, :, early_range],
                delta_rows[:, :, early_range],
                pos_early,
                key_rows,
                value_rows,
                pos_keys,
            )

        def without_early(unused):
            return (zero_query, jnp.zeros((key_block, kv_width), jnp.float32))

        early_query, early_kv = lax.cond(block_idx < early_limit, with_early, without_early, 0)
        kv_low = (late_kv + early_kv).astype(jnp.bfloat16)
        grad_low = grad_low.at[slot_rows].set(kv_low.reshape(per_block, HALF, kv_width))
        return (early_sum + early_query, late_sum + late_query, grad_low)

    start_low = jnp.zeros((span_count, HALF, kv_width), jnp.bfloat16)
    early_sum, late_sum, grad_low = lax.fori_loop(
        0, late_limit, block_step, (zero_query, zero_query, start_low)
    )
    query_total = jnp.concatenate([early_sum, late_sum], axis=0)
    kv_flat = grad_low.reshape(length_all, kv_width)
    own_kv = summed_rows(kv_flat, CTX, 0).astype(jnp.float32)
    kv_low = own_kv.astype(jnp.bfloat16)
    query_grad = query_total.reshape(ROWS, H * DH).astype(jnp.bfloat16)
    gathered_adapter = gathered_copies(adapter.astype(jnp.bfloat16), "dp", 1)
    down_low = gathered_adapter[:, :D]
    up_low = gathered_adapter[:, D:]
    input_rows = hidden_in[0]
    mixed_up = lax.dot_general(
        kv_low, up_low, (((1,), (1,)), ((), ())), preferred_element_type=jnp.float32
    ).astype(jnp.bfloat16)
    mixed_down = lax.dot_general(
        input_rows, down_low, (((1,), (1,)), ((), ())), preferred_element_type=jnp.float32
    ).astype(jnp.bfloat16)
    grad_down = lax.dot_general(
        mixed_up, input_rows, (((0,), (0,)), ((), ())), preferred_element_type=jnp.float32
    )
    grad_up = lax.dot_general(
        mixed_down, kv_low, (((0,), (0,)), ((), ())), preferred_element_type=jnp.float32
    )
    grad_partial = jnp.concatenate([grad_down, grad_up], axis=1)
    grad_shard = summed_on_arrival(grad_partial.astype(jnp.bfloat16), "dp", 1)
    grad_shard = of_everyone(grad_shard, CTX)
    squares = of_everyone(jnp.sum(grad_shard * grad_shard), "dp")
    clip_factor = jnp.minimum(1.0, 1.0 / jnp.sqrt(squares + 1e-06))
    scaled = grad_shard * clip_factor
    moment_new = 0.9 * moment_first + 0.1 * scaled
    second_new = 0.999 * moment_second + 0.001 * scaled * scaled
    adapter_step = moment_new / BIAS_ONE / (jnp.sqrt(second_new / BIAS_TWO) + 1e-08)
    return (query_grad[None], kv_low[None], adapter_step)


def solution(mesh):
    torus = Mesh(mesh.devices.reshape(mesh.shape["dp"], 16, 2), ("dp", "ctx_0", "ctx_1"))
    placed = (
        P("dp", None),
        P("dp", CTX, None),
        P("dp", CTX, None),
        P("dp", CTX, None),
        P("dp", CTX, None),
        P("dp", CTX, None),
        P("dp", CTX, None),
        P("dp", CTX, None),
        P(None, "dp"),
        P(None, "dp"),
        P(None, "dp"),
    )
    return jax.shard_map(
        per_device,
        mesh=torus,
        in_specs=placed,
        out_specs=(P("dp", CTX, None), P("dp", CTX, None), P(None, "dp")),
        check_vma=False,
    )
```

profile of v0, /device:TPU:6, one launch (start us, length us, event | category | flops | bytes accessed | tf_op | source)
XLA Modules:
  0.0 617.8 jit_solution(5849701136254166316)
XLA Ops:
  17.8 188.5 %all-gather.2.cloned.1.call-done = bf16[4096,1024]{1,0:T(8,128)(2,1)} async-done(((bf16[128,1024]{1,0:T(8,128)(2,1)}), bf16[4096,1024]{1,0:T(8,128)(2,1)}) %all-gather.2.cloned.1.call-update) | async-done | bytes 8388624 | tf_op jit(solution)/shard_map/all_gather | solution.py:22
  206.4 5.7 fusion.45
  212.1 6.9 %reshape.96 = bf16[64,64,4,128]{3,2,1,0:T(4,128)(2,1)} reshape(bf16[4096,512]{1,0:T(8,128)(2,1)} %get-tuple-element.268) | data formatting | bytes 8388608 | tf_op jit(solution)/shard_map/reshape | solution.py:135
  219.0 6.9 %reshape.97 = bf16[64,64,4,128]{3,2,1,0:T(4,128)(2,1)} reshape(bf16[4096,512]{1,0:T(8,128)(2,1)} %get-tuple-element.267) | data formatting | bytes 8388608 | tf_op jit(solution)/shard_map/reshape | solution.py:136
  227.7 4.3 broadcast_in_dim.75
  231.9 180.5 %while.15 = (s32[]{:T(128)}, f32[64,4,4,128]{3,0,2,1:T(8,128)}, f32[64,4,4,128]{3,0,2,1:T(8,128)}, bf16[64,64,1024]{2,1,0:T(8,128)(2,1)}, s32[]{:T(128)}, /*inde...) while((s32[]{:T(128)}, f32[64,4,4,128]{3,0,2,1:T(8,128)}, ...), condition=%wide.region_6.7_spmd.clone, body=%wide.region_2.6_spmd.clone.sunk | while | flops 1352730880 | bytes 67315992 | solution.py:191
  232.0 3.2 gather_fusion
  240.3 5.4 conditional.3
  259.1 3.2 gather_fusion
  263.2 3.2 gather_fusion.1
  281.0 3.2 gather_fusion
  285.2 3.2 gather_fusion.1
  303.0 3.2 gather_fusion
  307.1 3.2 gather_fusion.1
  324.9 3.2 gather_fusion
  329.0 3.2 gather_fusion.1
  412.5 102.2 %reduce-scatter.3.cloned.1.call-done = bf16[256,1024]{1,0:T(8,128)(2,1)} async-done(((bf16[4096,1024]{1,0:T(8,128)(2,1)}), bf16[256,1024]{1,0:T(8,128)(2,1)}) %reduce-scatter.3.cloned.1.call-update) | async-done | bytes 524304 | tf_op jit(solution)/shard_map/reduce_scatter | solution.py:32
  514.8 10.5 %all_to_all.21 = bf16[16,8,320]{2,1,0:T(8,128)(2,1)S(1)} all-to-all(bf16[16,8,320]{2,1,0:T(8,128)(2,1)S(1)} %broadcast_in_dim.81), channel_id=1, replica_groups=mesh['dp'=16,'ctx_0'=16,'ctx_1'=2] {'dp'}, dimensions={0} | all-to-all | bytes 163840 | tf_op jit(solution)/shard_map/all_to_all | solution.py:44
  525.5 15.4 %reduce-scatter.5.cloned.1.call-done = bf16[128,1024]{1,0:T(8,128)(2,1)} async-done(((bf16[256,1024]{1,0:T(8,128)(2,1)}), bf16[128,1024]{1,0:T(8,128)(2,1)}) %reduce-scatter.5.cloned.1.call-update) | async-done | bytes 262160 | tf_op jit(solution)/shard_map/reduce_scatter | solution.py:32
  544.2 10.5 %all_to_all.22 = bf16[16,8,320]{2,1,0:T(8,128)(2,1)S(1)} all-to-all(bf16[16,8,320]{2,1,0:T(8,128)(2,1)S(1)} %bitcast.183), channel_id=1, replica_groups=mesh['dp'=16,'ctx_0'=16,'ctx_1'=2] {'dp'}, dimensions={0} | all-to-all | bytes 163840 | tf_op jit(solution)/shard_map/all_to_all | solution.py:61
  555.5 15.3 %all-to-all-start.2 = ((f32[32,8,320]{2,1,0:T(8,128)}), f32[32,8,320]{2,1,0:T(8,128)S(1)}, u32[]{:S(2)}, u32[]{:S(2)}) async-start(f32[32,8,320]{2,1,0:T(8,128)} %broadcast_in_dim.82), calls=%async_computation.4 | async-start | bytes 786432 | tf_op jit(solution)/shard_map/all_to_all | solution.py:44
  571.4 26.8 %all-to-all-done.2 = f32[32,8,320]{2,1,0:T(8,128)S(1)} async-done(((f32[32,8,320]{2,1,0:T(8,128)}), f32[32,8,320]{2,1,0:T(8,128)S(1)}, u32[]{:S(2)}, u32[]{:S(2)}) %all-to-all-start.2) | async-done | bytes 327712 | tf_op jit(solution)/shard_map/all_to_all | solution.py:44
  600.1 4.6 all-to-all-start.3
  605.9 3.5 all-to-all-done.3
  (337 shorter events, 171.4 us)
Async XLA Ops:
  7.2 533.7 %copy-start = (bf16[1,128,4096]{2,1,0:T(8,128)(2,1)S(1)}, bf16[1,128,4096]{2,1,0:T(8,128)(2,1)}, u32[]{:S(2)}) copy-start(bf16[1,128,4096]{2,1,0:T(8,128)(2,1)} %param.16) | copy-start | bytes 3145732
  7.2 8.5 %copy-start.11 = (bf16[1,128,2048]{2,1,0:T(8,128)(2,1)S(1)}, bf16[1,128,2048]{2,1,0:T(8,128)(2,1)}, u32[]{:S(2)}) copy-start(bf16[1,128,2048]{2,1,0:T(8,128)(2,1)} %param.21) | copy-start | bytes 1572868
  7.2 199.2 %all-gather.2.cloned.1.call-start = ((), (), s32[]{:S(2)}) async-start(), calls=%async_computation.6 | async-start | bytes 8650752 | tf_op jit(solution)/shard_map/all_gather | solution.py:22
  9.1 505.7 %reduce-scatter.3.cloned.1.call-start = ((), (), s32[]{:S(2)}) async-start(), calls=%async_computation.7 | async-start | bytes 8912896 | tf_op jit(solution)/shard_map/reduce_scatter | solution.py:32
  13.2 3.7 copy-start.13
  227.7 4.3 copy-start.12
  240.3 1.9 copy-start.4
  247.6 1.9 copy-start.3
  269.6 1.9 copy-start.3
  291.5 1.9 copy-start.3
  313.4 1.9 copy-start.3
  335.3 1.9 copy-start.3
  337.2 1.6 copy-start.1
  357.3 1.9 copy-start.3
  379.2 1.9 copy-start.3
  401.1 1.9 copy-start.3
  412.5 102.3 %copy-start.14 = (f32[8,320]{1,0:T(8,128)S(1)}, f32[8,320]{1,0:T(8,128)}, u32[]{:S(2)}) copy-start(f32[8,320]{1,0:T(8,128)} %param.23) | copy-start | bytes 30724
  412.5 128.4 %reduce-scatter.5.cloned.1.call-start = ((), (), s32[]{:S(2)}) async-start(), calls=%async_computation.8 | async-start | bytes 786432 | tf_op jit(solution)/shard_map/reduce_scatter | solution.py:32
  525.5 45.3 %copy-start.8 = (f32[64,4,4,128]{3,0,2,1:T(8,128)S(1)}, f32[64,4,4,128]{3,0,2,1:T(8,128)}, u32[]{:S(2)}) copy-start(f32[64,4,4,128]{3,0,2,1:T(8,128)} %get-tuple-element.115) | copy-start | bytes 1572868
  542.4 28.4 %copy-start.5 = (f32[64,4,4,128]{3,0,2,1:T(8,128)S(1)}, f32[64,4,4,128]{3,0,2,1:T(8,128)}, u32[]{:S(2)}) copy-start(f32[64,4,4,128]{3,0,2,1:T(8,128)} %get-tuple-element.114) | copy-start | bytes 1572868
  555.5 42.7 %all-to-all-start.2 = ((f32[32,8,320]{2,1,0:T(8,128)}), f32[32,8,320]{2,1,0:T(8,128)S(1)}, u32[]{:S(2)}, u32[]{:S(2)}) async-start(f32[32,8,320]{2,1,0:T(8,128)} %broadcast_in_dim.82), calls=%async_computation.4 | async-start | bytes 786432 | tf_op jit(solution)/shard_map/all_to_all | solution.py:44
  570.9 39.8 %copy-start.15 = (f32[8,320]{1,0:T(8,128)S(1)}, f32[8,320]{1,0:T(8,128)}, u32[]{:S(2)}) copy-start(f32[8,320]{1,0:T(8,128)} %param.25) | copy-start | bytes 30724
  570.9 39.8 %copy-start.16 = (f32[8,320]{1,0:T(8,128)S(1)}, f32[8,320]{1,0:T(8,128)}, u32[]{:S(2)}) copy-start(f32[8,320]{1,0:T(8,128)} %param.24) | copy-start | bytes 30724
  600.1 9.3 %all-to-all-start.3 = ((f32[16,1,1]{2,1,0:T(1,128)}), f32[16,1,1]{2,1,0:T(1,128)S(1)}, u32[]{:S(2)}, u32[]{:S(2)}) async-start(f32[16,1,1]{2,1,0:T(1,128)} %broadcast_in_dim.83), calls=%async_computation.5 | async-start | bytes 16384 | tf_op jit(solution)/shard_map/all_to_all | solution.py:44
  (34 other events, 50.1 us)
Sparse Core Ops, SparseCore 0:
  11.7 194.6 all-gather.1
  412.6 102.1 reduce-scatter.2
  518.1 22.7 reduce-scatter.4
where the time goes:
time: 622 us; the launch traced here: 618 us
  waiting for transfers between devices  337 us (54%)
  local copies, waits for them, and re-layouts  146 us (23%)
  matrix products  43.2 us (7%)
  other arithmetic  32.3 us (5%)
  blocking collectives  21 us (3%)
  starting transfers between devices  20 us (3%)
  between operations  17.4 us (3%)
    all_gather x1, waiting for transfers between devices, in_one_piece(): lax.all_gather(both, axis, axis=dim, tiled=True)  189 us
    reduce_scatter x2, waiting for transfers between devices, summed_rows(): nearer = lax.psum_scatter(shard, axes[0], scatter_dimension=dim, tiled=True)  118 us
    gather x16, local copies, waits for them, and re-layouts, block_step(): key_rows = span_keys[slot_rows].reshape(key_block, KVH, DH)  32.9 us
    gather x16, local copies, waits for them, and re-layouts, block_step(): value_rows = span_values[slot_rows].reshape(key_block, KVH, DH)  32.8 us
    all_to_all x2, waiting for transfers between devices, from_everyone(): lax.all_to_all(jnp.broadcast_to(shard[None], (count, *shard.shape)), axis...  30.3 us
    scatter x8, local copies, waits for them, and re-layouts, block_step(): grad_low.at[slot_rows].set(kv_low.reshape(per_block, HALF, kv_width))  23.1 us
    all_to_all x2, starting transfers between devices, from_everyone(): lax.all_to_all(jnp.broadcast_to(shard[None], (count, *shard.shape)), axis...  19.9 us
    add x8, other arithmetic, block_step(): return (early_sum + early_query, late_sum + late_query, grad_low)  15.3 us
  transfers between devices with their start and end apart: 5, of which 5 were waited for; matrix products, arithmetic and copies ran while one was open for 1% of the time, Pallas kernels for 0%

commit v1 on v0

v1 whole, which is shorter than its diff:
```python
import jax
import jax.numpy as jnp
from jax import lax
from jax.experimental import pallas as pl
from jax.experimental.pallas import tpu as pltpu
from jax.sharding import Mesh
from jax.sharding import PartitionSpec as P

D = 4096
H = 16
KVH = 4
DH = 128
ROWS = 128
HALF = 64
GROUP = H // KVH
KEY_BLOCK = 256
SCALE = DH ** (-0.5)
CTX = ("ctx_0", "ctx_1")
PAIR = ((0, 1), (1, 0))


BIAS_ONE = 1.0 - 0.9**100.0
BIAS_TWO = 1.0 - 0.999**100.0


def prepare_kernel(q_mine, g_mine, q_other, g_other, q_out, g_out, qt_out, gt_out):
    halves = ROWS // HALF
    for j in range(KVH):
        for s in range(2 * halves):
            place = j * 2 * halves + s
            for source, rows_out, cols_out in (
                ((q_mine, q_other)[s // halves], q_out, qt_out),
                ((g_mine, g_other)[s // halves], g_out, gt_out),
            ):
                first = (s % halves) * HALF
                pieces = [
                    source[first : first + HALF, (j * GROUP + g) * DH : (j * GROUP + g + 1) * DH]
                    for g in range(GROUP)
                ]
                rows = jnp.concatenate(pieces, axis=0)
                rows_out[place] = rows
                cols_out[place] = rows.T


def prepared(q_mine, g_mine, q_other, g_other):
    count = KVH * 2 * ROWS // HALF
    vmem = pl.BlockSpec(memory_space=pltpu.VMEM)
    tall = jax.ShapeDtypeStruct((count, GROUP * HALF, DH), jnp.bfloat16)
    wide = jax.ShapeDtypeStruct((count, DH, GROUP * HALF), jnp.bfloat16)
    return pl.pallas_call(
        prepare_kernel,
        out_shape=(tall, tall, wide, wide),
        in_specs=[vmem] * 4,
        out_specs=(vmem,) * 4,
        compiler_params=pltpu.CompilerParams(vmem_limit_bytes=24 * 1024 * 1024),
    )(q_mine, g_mine, q_other, g_other)


def attention_kernel(
    table_ref, kv_ref, q_s, g_s, qt_s, gt_s, stat_ref,
    dq_ref, dkv_ref,
    k_s, v_s, kt_s, dk_s, dv_s, dqt_s,
):
    n_blocks = k_s.shape[1]
    n_spans = q_s.shape[0] // KVH
    pos_at = k_s.shape[1] * (KEY_BLOCK // HALF)
    span_at = 2 * pos_at
    less_at = span_at + n_spans
    seen_at = less_at + n_spans
    per_block = KEY_BLOCK // HALF
    n_rows = GROUP * HALF
    value_at = KVH * DH

    def arrange(b, carry):
        for i in range(per_block):
            row = pl.multiple_of(table_ref[b * per_block + i] * HALF, HALF)
            for j in range(KVH):
                k_s[j, b, pl.ds(i * HALF, HALF), :] = kv_ref[pl.ds(row, HALF), j * DH : (j + 1) * DH]
                v_s[j, b, pl.ds(i * HALF, HALF), :] = kv_ref[
                    pl.ds(row, HALF), value_at + j * DH : value_at + (j + 1) * DH
                ]
        for j in range(KVH):
            kt_s[j, b] = k_s[j, b].T
            dk_s[j, b] = jnp.zeros((KEY_BLOCK, DH), jnp.float32)
            dv_s[j, b] = jnp.zeros((KEY_BLOCK, DH), jnp.float32)
        return carry

    lax.fori_loop(0, n_blocks, arrange, 0)

    def tiles(n, j, s, blocks, masked):
        norm = stat_ref[0, pl.ds(n, 1), :]
        delta = stat_ref[1, pl.ds(n, 1), :]
        low, d_low = [], []
        for b in blocks:
            scores = jnp.dot(k_s[j, b], qt_s[n], preferred_element_type=jnp.float32) * SCALE
            weights = jnp.exp(scores - norm)
            if masked:
                lane = lax.broadcasted_iota(jnp.int32, (HALF, n_rows), 1)
                line = lax.broadcasted_iota(jnp.int32, (HALF, n_rows), 0)
                ahead = line - lax.rem(lane, HALF)
                shifts = [(table_ref[span_at + s] - table_ref[pos_at + b * per_block + i]) * HALF for i in range(per_block)]
                weights = jnp.concatenate(
                    [
                        jnp.where(ahead <= shifts[i], weights[i * HALF : (i + 1) * HALF], 0.0)
                        for i in range(per_block)
                    ],
                    axis=0,
                )
            d_weights = jnp.dot(v_s[j, b], gt_s[n], preferred_element_type=jnp.float32)
            low.append(weights.astype(jnp.bfloat16))
            d_low.append((weights * (d_weights - delta)).astype(jnp.bfloat16))
        total = None
        value_terms = [jnp.dot(w, g_s[n], preferred_element_type=jnp.float32) for w in low]
        key_terms = [jnp.dot(d, q_s[n], preferred_element_type=jnp.float32) for d in d_low]
        for b, d in zip(blocks, d_low):
            term = jnp.dot(kt_s[j, b], d, preferred_element_type=jnp.float32)
            total = term if total is None else total + term
        for b, term in zip(blocks, value_terms):
            dv_s[j, b] += term
        for b, term in zip(blocks, key_terms):
            dk_s[j, b] += term
        dqt_s[...] += total

    def query_span(n, carry):
        j = n // n_spans
        s = lax.rem(n, n_spans)
        whole = table_ref[less_at + s] // per_block
        dqt_s[...] = jnp.zeros(dqt_s.shape, jnp.float32)

        def pair(i, c):
            tiles(n, j, s, (2 * i, 2 * i + 1), False)
            return c

        lax.fori_loop(0, whole // 2, pair, 0)

        @pl.when(lax.rem(whole, 2) == 1)
        def _():
            tiles(n, j, s, (whole - 1,), False)

        @pl.when(table_ref[seen_at + s] > whole * per_block)
        def _():
            tiles(n, j, s, (whole,), True)

        total = (dqt_s[...] * SCALE).T
        row = pl.multiple_of(s * HALF, HALF)
        for g in range(GROUP):
            col = pl.multiple_of((j * GROUP + g) * DH, DH)
            dq_ref[pl.ds(row, HALF), pl.ds(col, DH)] = total[g * HALF : (g + 1) * HALF]
        return carry

    lax.fori_loop(0, KVH * n_spans, query_span, 0)

    def give_back(b, carry):
        for i in range(per_block):
            row = pl.multiple_of(table_ref[b * per_block + i] * HALF, HALF)
            for j in range(KVH):
                rows = pl.ds(i * HALF, HALF)
                dkv_ref[pl.ds(row, HALF), j * DH : (j + 1) * DH] = (dk_s[j, b, rows, :] * SCALE).astype(jnp.bfloat16)
                dkv_ref[pl.ds(row, HALF), value_at + j * DH : value_at + (j + 1) * DH] = dv_s[j, b, rows, :].astype(
                    jnp.bfloat16
                )
        return carry

    lax.fori_loop(0, n_blocks, give_back, 0)


def attention_terms(table, kv, prepared_rows, stats):
    length = kv.shape[0]
    n_blocks = length // KEY_BLOCK
    n_spans = prepared_rows[0].shape[0] // KVH
    smem = pl.BlockSpec(memory_space=pltpu.SMEM)
    vmem = pl.BlockSpec(memory_space=pltpu.VMEM)
    bf, f32 = jnp.bfloat16, jnp.float32
    return pl.pallas_call(
        attention_kernel,
        out_shape=(
            jax.ShapeDtypeStruct((n_spans * HALF, H * DH), f32),
            jax.ShapeDtypeStruct(kv.shape, bf),
        ),
        in_specs=[smem] + [vmem] * 6,
        out_specs=(vmem, vmem),
        scratch_shapes=[
            pltpu.VMEM((KVH, n_blocks, KEY_BLOCK, DH), bf),
            pltpu.VMEM((KVH, n_blocks, KEY_BLOCK, DH), bf),
            pltpu.VMEM((KVH, n_blocks, DH, KEY_BLOCK), bf),
            pltpu.VMEM((KVH, n_blocks, KEY_BLOCK, DH), f32),
            pltpu.VMEM((KVH, n_blocks, KEY_BLOCK, DH), f32),
            pltpu.VMEM((DH, GROUP * HALF), f32),
        ],
        compiler_params=pltpu.CompilerParams(vmem_limit_bytes=30 * 1024 * 1024),
    )(table, kv, *prepared_rows, stats)


def from_everyone(shard, axis):
    count = lax.axis_size(axis)
    return lax.all_to_all(
        jnp.broadcast_to(shard[None], (count, *shard.shape)), axis, 0, 0, tiled=True
    )


def swapped(block):
    return lax.ppermute(block, "ctx_1", PAIR)


def stat_rows(stats):
    tall = stats.reshape(ROWS // HALF, HALF, KVH, GROUP)
    return jnp.transpose(tall, (2, 0, 3, 1)).reshape(KVH, ROWS // HALF, GROUP * HALF)


def span_tables(span_ids):
    me_x = lax.axis_index("ctx_1")
    places = span_ids.reshape(lax.axis_size("ctx_0"), 2, ROWS // HALF)
    key_spans = lax.dynamic_index_in_dim(places, me_x, 1, keepdims=False).reshape(-1)
    here = lax.dynamic_index_in_dim(places, lax.axis_index("ctx_0"), 0, keepdims=False)
    own = lax.dynamic_index_in_dim(here, me_x, 0, keepdims=False)
    other = lax.dynamic_index_in_dim(here, 1 - me_x, 0, keepdims=False)
    spans = jnp.concatenate([own, other])
    count = key_spans.shape[0]
    slots = jnp.arange(count, dtype=jnp.int32)
    rank = jnp.sum((key_spans[None, :] < key_spans[:, None]).astype(jnp.int32), axis=1)
    at_rank = rank[None, :] == slots[:, None]
    slot_of = jnp.sum(jnp.where(at_rank, slots[None, :], 0), axis=1)
    pos_of = jnp.sum(jnp.where(at_rank, key_spans[None, :], 0), axis=1)
    less = jnp.sum((key_spans[None, :] < spans[:, None]).astype(jnp.int32), axis=1)
    seen = jnp.sum((key_spans[None, :] <= spans[:, None]).astype(jnp.int32), axis=1)
    return jnp.concatenate([slot_of, pos_of, spans, less, seen])


def per_device(
    span_ids,
    hidden_in,
    queries,
    keys_in,
    values_in,
    attn_out,
    out_grad,
    log_norm,
    adapter,
    moment_first,
    moment_second,
):
    f32, low = jnp.float32, jnp.bfloat16
    z_count = lax.axis_size("ctx_0")
    dp_count = lax.axis_size("dp")
    width = adapter.shape[1]
    query_rows, grad_rows, input_rows = queries[0], out_grad[0], hidden_in[0]

    kv_rows = jnp.concatenate([keys_in[0], values_in[0]], axis=1)
    kv_all = lax.all_gather(kv_rows, "ctx_0", axis=0, tiled=True)

    query_other = swapped(query_rows)
    grad_other = swapped(grad_rows)
    products = grad_rows.astype(f32) * attn_out[0].astype(f32)
    delta = jnp.sum(products.reshape(ROWS, H, DH), axis=-1)
    own_stats = jnp.stack([stat_rows(log_norm[0]), stat_rows(delta)])
    stats = jnp.concatenate([own_stats, swapped(own_stats)], axis=2)
    stats = stats.reshape(2, 2 * KVH * ROWS // HALF, GROUP * HALF)
    table = span_tables(span_ids[0])
    prepared_rows = prepared(query_rows, grad_rows, query_other, grad_other)

    adapter_low = from_everyone(adapter.astype(low), "dp")
    adapter_low = jnp.transpose(adapter_low, (1, 0, 2)).reshape(adapter.shape[0], dp_count * width)
    mixed_down = lax.dot_general(
        adapter_low[:, :D], input_rows, (((1,), (1,)), ((), ())), preferred_element_type=f32
    ).astype(low)
    mixed_down = from_everyone(mixed_down, "ctx_0")
    mixed_down = jnp.transpose(mixed_down, (1, 0, 2)).reshape(adapter.shape[0], z_count * ROWS)

    prepared_rows, mixed_down, adapter_low = lax.optimization_barrier(
        (prepared_rows, mixed_down, adapter_low)
    )
    query_terms, kv_part = attention_terms(table, kv_all, prepared_rows, stats)
    kv_low = lax.psum_scatter(kv_part, "ctx_0", scatter_dimension=0, tiled=True)

    query_total = query_terms[:ROWS] + swapped(query_terms[ROWS:].astype(low)).astype(f32)
    query_grad = query_total.astype(low)

    up_terms = lax.dot_general(
        adapter_low[:, D:], kv_part, (((1,), (1,)), ((), ())), preferred_element_type=f32
    )
    up_terms = jnp.transpose(up_terms.reshape(adapter.shape[0], z_count, ROWS), (1, 0, 2))
    mixed_up = lax.all_to_all(up_terms, "ctx_0", 0, 0, tiled=True).sum(axis=0).astype(low)
    grad_up = jnp.dot(mixed_down, kv_part, preferred_element_type=f32)
    grad_down = jnp.dot(mixed_up, input_rows, preferred_element_type=f32)
    grad_partial = jnp.concatenate([grad_down, grad_up], axis=1).astype(low)
    pieces = jnp.transpose(grad_partial.reshape(adapter.shape[0], dp_count, width), (1, 0, 2))
    pieces = jnp.broadcast_to(pieces[:, None], (dp_count, 2, *adapter.shape))
    pieces = pieces.reshape(2 * dp_count, *adapter.shape)
    arrived = lax.all_to_all(pieces, ("dp", "ctx_1"), 0, 0, tiled=True)
    grad_shard = arrived.astype(f32).sum(axis=0)
    grad_shard = from_everyone(grad_shard.astype(low), "ctx_0").astype(f32).sum(axis=0)
    squares = from_everyone(jnp.sum(grad_shard * grad_shard), "dp").sum(axis=0)
    clip_factor = jnp.minimum(1.0, 1.0 / jnp.sqrt(squares + 1e-06))
    scaled = grad_shard * clip_factor
    moment_new = 0.9 * moment_first + 0.1 * scaled
    second_new = 0.999 * moment_second + 0.001 * scaled * scaled
    adapter_step = moment_new / BIAS_ONE / (jnp.sqrt(second_new / BIAS_TWO) + 1e-08)
    return (query_grad[None], kv_low[None], adapter_step)


def solution(mesh):
    torus = Mesh(mesh.devices.reshape(mesh.shape["dp"], -1, 2), ("dp", "ctx_0", "ctx_1"))
    placed = (
        P("dp", None),
        P("dp", CTX, None),
        P("dp", CTX, None),
        P("dp", CTX, None),
        P("dp", CTX, None),
        P("dp", CTX, None),
        P("dp", CTX, None),
        P("dp", CTX, None),
        P(None, "dp"),
        P(None, "dp"),
        P(None, "dp"),
    )
    return jax.shard_map(
        per_device,
        mesh=torus,
        in_specs=placed,
        out_specs=(P("dp", CTX, None), P("dp", CTX, None), P(None, "dp")),
        check_vma=False,
    )
```

time: 622 us -> 219 us (0.35)
  waiting for transfers between devices: 337 us -> 72.2 us
  local copies, waits for them, and re-layouts: 146 us -> 20.4 us
  matrix products: 43.2 us -> 7.48 us
  starting transfers between devices: 20 us -> 50.7 us
  Pallas kernels: 0 us -> 26.2 us
  other arithmetic: 32.3 us -> 10.5 us
    all_gather x1, waiting for transfers between devices: 189 us -> 30.4 us  [per_device(): kv_all = lax.all_gather(kv_rows, 'ctx_0', axis=0, tiled=True)]
    reduce_scatter x2 -> x1, waiting for transfers between devices: 118 us -> 10.6 us  [per_device(): kv_low = lax.psum_scatter(kv_part, 'ctx_0', scatter_dimension=0, tiled=True)]
    gather x32 -> x0, local copies, waits for them, and re-layouts: 65.7 us -> none  [the longest x16 32.9 us: block_step(): key_rows = span_keys[slot_rows].reshape(key_block, KVH, DH)]
    dot_general x47 -> x4, matrix products: 43.2 us -> 7.48 us  [the longest x1 4.01 us: per_device(): lax.dot_general(adapter_low[:, D:], kv_part, (((1,), (1,)), ((), ())), pr...]
    pallas_call x0 -> x2, Pallas kernels: none -> 26.2 us  [the longest x1 25.5 us: attention_terms(): pl.pallas_call(attention_kernel, out_shape=(jax.ShapeDtypeStruct((n_spans...]
    scatter x8 -> x0, local copies, waits for them, and re-layouts: 23.1 us -> none  [block_step(): grad_low.at[slot_rows].set(kv_low.reshape(per_block, HALF, kv_width))]
    ppermute x0 -> x4, starting transfers between devices: none -> 17.9 us  [swapped(): return lax.ppermute(block, 'ctx_1', PAIR)]
    add x26 -> x0, other arithmetic: 15.4 us -> none  [the longest x8 15.3 us: block_step(): return (early_sum + early_query, late_sum + late_query, grad_low)]
  transfers between devices with their start and end apart: 5 -> 11, of which waited for: 5 -> 6; matrix products, arithmetic and copies ran while one was open for 1% -> 11% of each run, Pallas kernels for 0% -> 0%
where the time goes in v1:
time: 219 us; the launch traced here: 217 us
  waiting for transfers between devices  72.2 us (33%)
  starting transfers between devices  50.7 us (23%)
  Pallas kernels  26.2 us (12%)
  local copies, waits for them, and re-layouts  20.4 us (9%)
  between operations  15.1 us (7%)
  blocking collectives  14.8 us (7%)
  other arithmetic  10.5 us (5%)
  matrix products  7.48 us (3%)
    all_gather x1, waiting for transfers between devices, per_device(): kv_all = lax.all_gather(kv_rows, 'ctx_0', axis=0, tiled=True)  30.4 us
    pallas_call x1, Pallas kernels, attention_terms(): pl.pallas_call(attention_kernel, out_shape=(jax.ShapeDtypeStruct((n_spans...  25.5 us
    all_to_all x4, starting transfers between devices, from_everyone(): lax.all_to_all(jnp.broadcast_to(shard[None], (count, *shard.shape)), axis...  25 us
    all_to_all x4, waiting for transfers between devices, from_everyone(): lax.all_to_all(jnp.broadcast_to(shard[None], (count, *shard.shape)), axis...  21 us
    ppermute x4, starting transfers between devices, swapped(): return lax.ppermute(block, 'ctx_1', PAIR)  17.9 us
    all_to_all x1, blocking collectives, per_device(): arrived = lax.all_to_all(pieces, ('dp', 'ctx_1'), 0, 0, tiled=True)  14.8 us
    unnamed x35, local copies, waits for them, and re-layouts  14.7 us
    reduce_scatter x1, waiting for transfers between devices, per_device(): kv_low = lax.psum_scatter(kv_part, 'ctx_0', scatter_dimension=0, tiled=True)  10.6 us
  transfers between devices with their start and end apart: 11, of which 6 were waited for; matrix products, arithmetic and copies ran while one was open for 11% of the time, Pallas kernels for 0%

profile of v1, /device:TPU:6, one launch (start us, length us, event | category | flops | bytes accessed | tf_op | source)
XLA Modules:
  0.0 217.3 jit_solution(15468615207122521214)
XLA Ops:
  7.3 1.8 pad_maximum_fusion
  10.5 5.9 %all-to-all-start = ((bf16[16,8,320]{2,1,0:T(8,128)(2,1)}), bf16[16,8,320]{2,1,0:T(8,128)(2,1)S(1)}, u32[]{:S(2)}, u32[]{:S(2)}) async-start(bf16[16,8,320]{2,1,0:T(8,128)(2,1)} %broadcast_in_dim.32), calls=%async_computation | async-start | bytes 196608 | tf_op jit(solution)/shard_map/all_to_all | solution.py:196
  16.4 6.6 %collective-permute-start = (bf16[128,2048]{1,0:T(8,128)(2,1)}, bf16[128,2048]{1,0:T(8,128)(2,1)S(1)}, u32[]{:S(2)}, u32[]{:S(2)}) collective-permute-start(bf16[128,2048]{1,0:T(8,128)(2,1)} %bitcast.44), channel_id=1, source_target_pairs={{0,1},{1,0},{2,3},{3,2},{4,5},{5,4},{6,7},{7,6},{8,9},{9,8},{10,11... | collective-permute-start | bytes 1572872 | tf_op jit(solution)/shard_map/ppermute | solution.py:202
  23.0 1.9 collective-permute-start.1
  28.3 1.6 reduce_sum.107
  30.1 5.4 %collective-permute-start.2 = (f32[2,4,2,256]{3,2,1,0:T(2,128)S(1)}, f32[2,4,2,256]{3,2,1,0:T(2,128)S(1)}, u32[]{:S(2)}, u32[]{:S(2)}) collective-permute-start(f32[2,4,2,256]{3,2,1,0:T(2,128)S(1)} %constant_dynamic-update-slice_fusion), channel_id=1, source_target_pairs={{0,1},{1,0},{2,3},{3,2},{4,5},{5,4},{6,7},{7,6},{8,9},{9,8},{10,11... | collective-permute-start | bytes 49160 | tf_op jit(solution)/shard_map/ppermute | solution.py:202
  38.7 11.9 %all-to-all-start.1 = ((bf16[16,8,128]{2,1,0:T(8,128)(2,1)}), bf16[16,8,128]{2,1,0:T(8,128)(2,1)S(1)}, u32[]{:S(2)}, u32[]{:S(2)}) async-start(bf16[16,8,128]{2,1,0:T(8,128)(2,1)} %broadcast_in_dim.33), calls=%async_computation.1 | async-start | bytes 65536 | tf_op jit(solution)/shard_map/all_to_all | solution.py:196
  55.6 8.0 %all-to-all-done.1 = bf16[16,8,128]{2,1,0:T(8,128)(2,1)S(1)} async-done(((bf16[16,8,128]{2,1,0:T(8,128)(2,1)}), bf16[16,8,128]{2,1,0:T(8,128)(2,1)S(1)}, u32[]{:S(2)}, u32[]{:S(2)}) %all-to-all-start.1) | async-done | bytes 32800 | tf_op jit(solution)/shard_map/all_to_all | solution.py:196
  63.6 30.4 %all-gather.2.cloned.1.call-done.kv_ref = bf16[2048,1024]{1,0:T(8,128)(2,1)} async-done(((bf16[128,1024]{1,0:T(8,128)(2,1)}), bf16[2048,1024]{1,0:T(8,128)(2,1)}) %all-gather.2.cloned.1.call-update) | async-done | bytes 4194320 | tf_op jit(solution)/shard_map/all_gather | solution.py:249
  94.0 2.2 %copy-done.2 = bf16[2048,1024]{1,0:T(8,128)(2,1)S(1)} copy-done((bf16[2048,1024]{1,0:T(8,128)(2,1)S(1)}, bf16[2048,1024]{1,0:T(8,128)(2,1)}, u32[]{:S(2)}) %copy-start.2) | copy-done | bytes 4194328
  101.1 25.5 %shard_map.131 = (f32[256,2048]{1,0:T(8,128)S(1)}, bf16[2048,1024]{1,0:T(8,128)(2,1)S(1)}) custom-call(s32[76]{0:T(128)S(1)} %concatenate.18.table_ref, bf16[2048,1024]{1,0:T(8,128)(2,1)S(1)} %copy-done.2, bf16[16,256,128]{2,1,0:T(8,128)(2,1)S(1)} %copy-done.5, bf16[16,256,128]{2,1,0:T(8,128)(2,1)S(1)} %copy-done.7, bf16[16,128,256]{2,1,0:T(8,128)(2,1)S(1)} %copy-done.9, ...), custom_call_target="tpu_custom_call" | custom-call | tf_op jit(solution)/shard_map/pallas_call | solution.py:174
  126.6 1.9 copy-done.1
  128.5 4.0 %convolution_bitcast_fusion = f32[16,8,128]{2,1,0:T(8,128)} fusion(bf16[2048,1024]{1,0:T(8,128)(2,1)} %copy-done.1, bf16[8,5120]{1,0:T(8,128)(2,1)S(1)} %reshape.50), kind=kOutput, calls=%fused_computation.1 | convolution fusion | flops 33554432 | bytes 4276224 | tf_op jit(solution)/shard_map/dot_general | solution.py:278
  132.6 7.7 %all-to-all-start.2 = ((f32[16,8,128]{2,1,0:T(8,128)}), f32[16,8,128]{2,1,0:T(8,128)S(1)}, u32[]{:S(2)}, u32[]{:S(2)}) async-start(f32[16,8,128]{2,1,0:T(8,128)} %convolution_bitcast_fusion), calls=%async_computation.3 | async-start | bytes 131072 | tf_op jit(solution)/shard_map/all_to_all | solution.py:282
  140.3 2.8 %convolution_convert_fusion.1 = bf16[8,1024]{1,0:T(8,128)(2,1)S(1)} fusion(bf16[8,2048]{1,0:T(8,128)(2,1)S(1)} %bitcast.50, bf16[2048,1024]{1,0:T(8,128)(2,1)} %copy-done.1), kind=kOutput, calls=%fused_computation.2 | convolution fusion | flops 33562624 | bytes 4243456 | tf_op jit(solution)/shard_map/dot_general | solution.py:283
  143.1 10.1 %all-to-all-done.2 = f32[16,8,128]{2,1,0:T(8,128)S(1)} async-done(((f32[16,8,128]{2,1,0:T(8,128)}), f32[16,8,128]{2,1,0:T(8,128)S(1)}, u32[]{:S(2)}, u32[]{:S(2)}) %all-to-all-start.2) | async-done | bytes 65568 | tf_op jit(solution)/shard_map/all_to_all | solution.py:282
  153.7 14.8 %all_to_all.31 = bf16[32,8,320]{2,1,0:T(8,128)(2,1)S(1)} all-to-all(bf16[32,8,320]{2,1,0:T(8,128)(2,1)S(1)} %bitcast.47), channel_id=1, replica_groups=mesh['dp'=16,'ctx_0'=16,'ctx_1'=2] {'dp','ctx_1'}, dimensions={0} | all-to-all | bytes 327680 | tf_op jit(solution)/shard_map/all_to_all | solution.py:289
  169.2 3.5 %all-to-all-start.4 = ((bf16[16,8,320]{2,1,0:T(8,128)(2,1)}), bf16[16,8,320]{2,1,0:T(8,128)(2,1)S(1)}, u32[]{:S(2)}, u32[]{:S(2)}) async-start(bf16[16,8,320]{2,1,0:T(8,128)(2,1)} %broadcast_in_dim.64), calls=%async_computation.5 | async-start | bytes 196608 | tf_op jit(solution)/shard_map/all_to_all | solution.py:196
  173.5 4.0 %collective-permute-start.3 = (bf16[128,2048]{1,0:T(8,128)(2,1)}, bf16[128,2048]{1,0:T(8,128)(2,1)}, u32[]{:S(2)}, u32[]{:S(2)}) collective-permute-start(bf16[128,2048]{1,0:T(8,128)(2,1)} %slice.27), channel_id=1, source_target_pairs={{0,1},{1,0},{2,3},{3,2},{4,5},{5,4},{6,7},{7,6},{8,9},{9,8},{10,11... | collective-permute-start | bytes 1572872 | tf_op jit(solution)/shard_map/ppermute | solution.py:202
  177.5 10.2 %all-to-all-done.4 = bf16[16,8,320]{2,1,0:T(8,128)(2,1)S(1)} async-done(((bf16[16,8,320]{2,1,0:T(8,128)(2,1)}), bf16[16,8,320]{2,1,0:T(8,128)(2,1)S(1)}, u32[]{:S(2)}, u32[]{:S(2)}) %all-to-all-start.4) | async-done | bytes 81952 | tf_op jit(solution)/shard_map/all_to_all | solution.py:196
  189.5 3.7 %all-to-all-start.5 = ((f32[16,1,1]{2,1,0:T(1,128)}), f32[16,1,1]{2,1,0:T(1,128)S(1)}, u32[]{:S(2)}, u32[]{:S(2)}) async-start(f32[16,1,1]{2,1,0:T(1,128)} %broadcast_in_dim.65), calls=%async_computation.6 | async-start | bytes 16384 | tf_op jit(solution)/shard_map/all_to_all | solution.py:196
  193.2 1.9 fusion.2
  195.1 2.7 %all-to-all-done.5 = f32[16,1,1]{2,1,0:T(1,128)S(1)} async-done(((f32[16,1,1]{2,1,0:T(1,128)}), f32[16,1,1]{2,1,0:T(1,128)S(1)}, u32[]{:S(2)}, u32[]{:S(2)}) %all-to-all-start.5) | async-done | bytes 96 | tf_op jit(solution)/shard_map/all_to_all | solution.py:196
  199.8 10.6 %reduce-scatter.2.cloned.1.call-done = bf16[128,1024]{1,0:T(8,128)(2,1)} async-done(((bf16[2048,1024]{1,0:T(8,128)(2,1)}), bf16[128,1024]{1,0:T(8,128)(2,1)}) %reduce-scatter.2.cloned.1.call-update) | async-done | bytes 262160 | tf_op jit(solution)/shard_map/reduce_scatter | solution.py:273
  (84 shorter events, 22.9 us)
Async XLA Ops:
  7.2 30.5 %copy-start = (bf16[1,128,4096]{2,1,0:T(8,128)(2,1)S(1)}, bf16[1,128,4096]{2,1,0:T(8,128)(2,1)}, u32[]{:S(2)}) copy-start(bf16[1,128,4096]{2,1,0:T(8,128)(2,1)} %param.12) | copy-start | bytes 3145732
  7.2 28.9 %copy-start.15 = (s32[1,64]{1,0:T(1,128)S(1)}, s32[1,64]{1,0:T(1,128)}, u32[]{:S(2)}) copy-start(s32[1,64]{1,0:T(1,128)} %param.11) | copy-start | bytes 772
  7.2 86.8 %all-gather.2.cloned.1.call-start = ((), (), s32[]{:S(2)}) async-start(), calls=%async_computation.7 | async-start | bytes 4456448 | tf_op jit(solution)/shard_map/all_gather | solution.py:249
  7.2 43.7 %copy-start.3 = (bf16[1,128,2048]{2,1,0:T(8,128)(2,1)S(1)}, bf16[1,128,2048]{2,1,0:T(8,128)(2,1)}, u32[]{:S(2)}) copy-start(bf16[1,128,2048]{2,1,0:T(8,128)(2,1)} %param.17) | copy-start | bytes 1572868
  7.2 43.7 %copy-start.12 = (bf16[1,128,2048]{2,1,0:T(8,128)(2,1)S(1)}, bf16[1,128,2048]{2,1,0:T(8,128)(2,1)}, u32[]{:S(2)}) copy-start(bf16[1,128,2048]{2,1,0:T(8,128)(2,1)} %param.13) | copy-start | bytes 1572868
  10.5 27.0 %all-to-all-start = ((bf16[16,8,320]{2,1,0:T(8,128)(2,1)}), bf16[16,8,320]{2,1,0:T(8,128)(2,1)S(1)}, u32[]{:S(2)}, u32[]{:S(2)}) async-start(bf16[16,8,320]{2,1,0:T(8,128)(2,1)} %broadcast_in_dim.32), calls=%async_computation | async-start | bytes 196608 | tf_op jit(solution)/shard_map/all_to_all | solution.py:196
  16.4 34.5 %collective-permute-start = (bf16[128,2048]{1,0:T(8,128)(2,1)}, bf16[128,2048]{1,0:T(8,128)(2,1)S(1)}, u32[]{:S(2)}, u32[]{:S(2)}) collective-permute-start(bf16[128,2048]{1,0:T(8,128)(2,1)} %bitcast.44), channel_id=1, source_target_pairs={{0,1},{1,0},{2,3},{3,2},{4,5},{5,4},{6,7},{7,6},{8,9},{9,8},{10,11... | collective-permute-start | bytes 1572872 | tf_op jit(solution)/shard_map/ppermute | solution.py:202
  23.0 27.9 %collective-permute-start.1 = (bf16[128,2048]{1,0:T(8,128)(2,1)}, bf16[128,2048]{1,0:T(8,128)(2,1)S(1)}, u32[]{:S(2)}, u32[]{:S(2)}) collective-permute-start(bf16[128,2048]{1,0:T(8,128)(2,1)} %bitcast.42), channel_id=1, source_target_pairs={{0,1},{1,0},{2,3},{3,2},{4,5},{5,4},{6,7},{7,6},{8,9},{9,8},{10,11... | collective-permute-start | bytes 1572872 | tf_op jit(solution)/shard_map/ppermute | solution.py:202
  30.1 20.7 %collective-permute-start.2 = (f32[2,4,2,256]{3,2,1,0:T(2,128)S(1)}, f32[2,4,2,256]{3,2,1,0:T(2,128)S(1)}, u32[]{:S(2)}, u32[]{:S(2)}) collective-permute-start(f32[2,4,2,256]{3,2,1,0:T(2,128)S(1)} %constant_dynamic-update-slice_fusion), channel_id=1, source_target_pairs={{0,1},{1,0},{2,3},{3,2},{4,5},{5,4},{6,7},{7,6},{8,9},{9,8},{10,11... | collective-permute-start | bytes 49160 | tf_op jit(solution)/shard_map/ppermute | solution.py:202
  38.7 24.9 %all-to-all-start.1 = ((bf16[16,8,128]{2,1,0:T(8,128)(2,1)}), bf16[16,8,128]{2,1,0:T(8,128)(2,1)S(1)}, u32[]{:S(2)}, u32[]{:S(2)}) async-start(bf16[16,8,128]{2,1,0:T(8,128)(2,1)} %broadcast_in_dim.33), calls=%async_computation.1 | async-start | bytes 65536 | tf_op jit(solution)/shard_map/all_to_all | solution.py:196
  50.6 159.8 %reduce-scatter.2.cloned.1.call-start = ((), (), s32[]{:S(2)}) async-start(), calls=%async_computation.8 | async-start | bytes 4456448 | tf_op jit(solution)/shard_map/reduce_scatter | solution.py:273
  52.6 1.0 copy-start.6
  94.0 2.2 %copy-start.2 = (bf16[2048,1024]{1,0:T(8,128)(2,1)S(1)}, bf16[2048,1024]{1,0:T(8,128)(2,1)}, u32[]{:S(2)}) copy-start(bf16[2048,1024]{1,0:T(8,128)(2,1)} %all-gather.2.cloned.1.call-done.kv_ref) | copy-start | bytes 12582916
  96.2 1.2 copy-start.5
  97.4 1.2 copy-start.7
  98.7 1.2 copy-start.9
  99.9 1.2 copy-start.11
  126.6 1.9 copy-start.1
  132.6 20.7 %all-to-all-start.2 = ((f32[16,8,128]{2,1,0:T(8,128)}), f32[16,8,128]{2,1,0:T(8,128)S(1)}, u32[]{:S(2)}, u32[]{:S(2)}) async-start(f32[16,8,128]{2,1,0:T(8,128)} %convolution_bitcast_fusion), calls=%async_computation.3 | async-start | bytes 131072 | tf_op jit(solution)/shard_map/all_to_all | solution.py:282
  140.2 58.9 %copy-start.13 = (f32[8,320]{1,0:T(8,128)S(1)}, f32[8,320]{1,0:T(8,128)}, u32[]{:S(2)}) copy-start(f32[8,320]{1,0:T(8,128)} %param.21) | copy-start | bytes 30724
  140.3 58.9 %copy-start.14 = (f32[8,320]{1,0:T(8,128)S(1)}, f32[8,320]{1,0:T(8,128)}, u32[]{:S(2)}) copy-start(f32[8,320]{1,0:T(8,128)} %param.20) | copy-start | bytes 30724
  169.2 18.6 %all-to-all-start.4 = ((bf16[16,8,320]{2,1,0:T(8,128)(2,1)}), bf16[16,8,320]{2,1,0:T(8,128)(2,1)S(1)}, u32[]{:S(2)}, u32[]{:S(2)}) async-start(bf16[16,8,320]{2,1,0:T(8,128)(2,1)} %broadcast_in_dim.64), calls=%async_computation.5 | async-start | bytes 196608 | tf_op jit(solution)/shard_map/all_to_all | solution.py:196
  173.5 19.6 %collective-permute-start.3 = (bf16[128,2048]{1,0:T(8,128)(2,1)}, bf16[128,2048]{1,0:T(8,128)(2,1)}, u32[]{:S(2)}, u32[]{:S(2)}) collective-permute-start(bf16[128,2048]{1,0:T(8,128)(2,1)} %slice.27), channel_id=1, source_target_pairs={{0,1},{1,0},{2,3},{3,2},{4,5},{5,4},{6,7},{7,6},{8,9},{9,8},{10,11... | collective-permute-start | bytes 1572872 | tf_op jit(solution)/shard_map/ppermute | solution.py:202
  189.5 8.3 %all-to-all-start.5 = ((f32[16,1,1]{2,1,0:T(1,128)}), f32[16,1,1]{2,1,0:T(1,128)S(1)}, u32[]{:S(2)}, u32[]{:S(2)}) async-start(f32[16,1,1]{2,1,0:T(1,128)} %broadcast_in_dim.65), calls=%async_computation.6 | async-start | bytes 16384 | tf_op jit(solution)/shard_map/all_to_all | solution.py:196
  (3 other events, 3.0 us)
Sparse Core Ops, SparseCore 0:
  10.7 83.3 all-gather.1
  128.7 81.7 reduce-scatter.1

commit v2 on v1

v2 whole, which is shorter than its diff:
```python
import jax
import jax.numpy as jnp
from jax import lax
from jax.experimental import pallas as pl
from jax.experimental.pallas import tpu as pltpu
from jax.sharding import Mesh
from jax.sharding import PartitionSpec as P

D = 4096
H = 16
KVH = 4
DH = 128
ROWS = 128
HALF = 64
GROUP = H // KVH
KEY_BLOCK = 256
SCALE = DH ** (-0.5)
CTX = ("ctx_0", "ctx_1")
PAIR = ((0, 1), (1, 0))


BIAS_ONE = 1.0 - 0.9**100.0
BIAS_TWO = 1.0 - 0.999**100.0


def attention_kernel(
    table_ref, kv_hbm, q_mine, g_mine, q_other, g_other, stat_ref,
    dq_mine, dq_other, dkv_hbm,
    raw_s, kv_s, dk_s, dv_s, dkv_s, q_s, g_s, qt_s, gt_s, dqt_s, raw_sem, in_sem, out_sem,
):
    n_blocks = kv_s.shape[0]
    n_spans = q_s.shape[0] // KVH
    per_block = KEY_BLOCK // HALF
    n_rows = GROUP * HALF
    value_at = KVH * DH
    pos_at = n_blocks * per_block
    span_at = 2 * pos_at
    less_at = span_at + n_spans
    seen_at = less_at + n_spans

    sources = (q_mine, g_mine, q_other, g_other)
    raw_copies = [pltpu.make_async_copy(source, raw_s.at[i], raw_sem.at[i]) for i, source in enumerate(sources)]
    for copy in raw_copies:
        copy.start()

    def span_in(rank):
        row = pl.multiple_of(table_ref[rank] * HALF, HALF)
        place = pl.multiple_of(lax.rem(rank, per_block) * HALF, HALF)
        return pltpu.make_async_copy(
            kv_hbm.at[pl.ds(row, HALF), :], kv_s.at[rank // per_block, pl.ds(place, HALF), :], in_sem.at[rank]
        )

    def span_out(rank):
        row = pl.multiple_of(table_ref[rank] * HALF, HALF)
        place = pl.multiple_of(lax.rem(rank, per_block) * HALF, HALF)
        return pltpu.make_async_copy(
            dkv_s.at[rank // per_block, pl.ds(place, HALF), :], dkv_hbm.at[pl.ds(row, HALF), :], out_sem.at[rank]
        )

    def start_in(rank, carry):
        span_in(rank).start()
        return carry

    lax.fori_loop(0, pos_at, start_in, 0)
    for copy in raw_copies:
        copy.wait()

    halves = ROWS // HALF
    for j in range(KVH):
        for s in range(n_spans):
            first = (s % halves) * HALF
            for kind, rows_out, cols_out in ((0, q_s, qt_s), (1, g_s, gt_s)):
                source = raw_s.at[2 * (s // halves) + kind]
                rows = jnp.concatenate(
                    [
                        source[first : first + HALF, (j * GROUP + g) * DH : (j * GROUP + g + 1) * DH]
                        for g in range(GROUP)
                    ],
                    axis=0,
                )
                rows_out[j * n_spans + s] = rows
                cols_out[j * n_spans + s] = rows.T
            dqt_s[j * n_spans + s] = jnp.zeros((DH, n_rows), jnp.float32)

    def key_cols(j):
        return slice(j * DH, (j + 1) * DH)

    def value_cols(j):
        return slice(value_at + j * DH, value_at + (j + 1) * DH)

    def heads(b, s, masked):
        if masked:
            lane = lax.broadcasted_iota(jnp.int32, (HALF, n_rows), 1)
            line = lax.broadcasted_iota(jnp.int32, (HALF, n_rows), 0)
            ahead = line - lax.rem(lane, HALF)
            visible = jnp.concatenate(
                [
                    ahead <= (table_ref[span_at + s] - table_ref[pos_at + b * per_block + i]) * HALF
                    for i in range(per_block)
                ],
                axis=0,
            )
        def front(j):
            n = j * n_spans + s
            scores = jnp.dot(kv_s[b, :, key_cols(j)], qt_s[n], preferred_element_type=jnp.float32)
            d_weights = jnp.dot(kv_s[b, :, value_cols(j)], gt_s[n], preferred_element_type=jnp.float32)
            return scores, d_weights

        def middle(j, scores, d_weights):
            n = j * n_spans + s
            weights = jnp.exp(scores * SCALE - stat_ref[0, pl.ds(n, 1), :])
            if masked:
                weights = jnp.where(visible, weights, 0.0)
            d_scores = (weights * (d_weights - stat_ref[1, pl.ds(n, 1), :])).astype(jnp.bfloat16)
            return weights.astype(jnp.bfloat16), d_scores

        def back(j, weights_low, d_scores):
            n = j * n_spans + s
            dv_s[j] += jnp.dot(weights_low, g_s[n], preferred_element_type=jnp.float32)
            dk_s[j] += jnp.dot(d_scores, q_s[n], preferred_element_type=jnp.float32)
            dqt_s[n] += lax.dot_general(
                kv_s[b, :, key_cols(j)], d_scores, (((0,), (0,)), ((), ())), preferred_element_type=jnp.float32
            )

        fronts = front(0)
        for j in range(KVH):
            middles = middle(j, *fronts)
            if j + 1 < KVH:
                fronts = front(j + 1)
            back(j, *middles)

    def block(b, carry):
        for i in range(per_block):
            span_in(b * per_block + i).wait()
        for j in range(KVH):
            dk_s[j] = jnp.zeros((KEY_BLOCK, DH), jnp.float32)
            dv_s[j] = jnp.zeros((KEY_BLOCK, DH), jnp.float32)

        def query_span(s, c):
            whole = table_ref[less_at + s] >= (b + 1) * per_block

            @pl.when(whole)
            def _():
                heads(b, s, False)

            @pl.when(jnp.logical_and(jnp.logical_not(whole), table_ref[seen_at + s] > b * per_block))
            def _():
                heads(b, s, True)

            return c

        lax.fori_loop(0, n_spans, query_span, 0)
        for j in range(KVH):
            dkv_s[b, :, key_cols(j)] = (dk_s[j] * SCALE).astype(jnp.bfloat16)
            dkv_s[b, :, value_cols(j)] = dv_s[j].astype(jnp.bfloat16)
        for i in range(per_block):
            span_out(b * per_block + i).start()
        return carry

    lax.fori_loop(0, n_blocks, block, 0)

    for j in range(KVH):
        for s in range(n_spans):
            total = (dqt_s[j * n_spans + s] * SCALE).T
            for g in range(GROUP):
                cols = slice((j * GROUP + g) * DH, (j * GROUP + g + 1) * DH)
                first = (s % halves) * HALF
                out = (dq_mine, dq_other)[s // halves]
                out[first : first + HALF, cols] = total[g * HALF : (g + 1) * HALF].astype(out.dtype)

    def finish_out(rank, carry):
        span_out(rank).wait()
        return carry

    lax.fori_loop(0, pos_at, finish_out, 0)


def attention_terms(table, kv, q_mine, g_mine, q_other, g_other, stats):
    length = kv.shape[0]
    n_blocks = length // KEY_BLOCK
    n_slots = length // HALF
    n_spans = 2 * ROWS // HALF
    count = KVH * n_spans
    smem = pl.BlockSpec(memory_space=pltpu.SMEM)
    vmem = pl.BlockSpec(memory_space=pltpu.VMEM)
    hbm = pl.BlockSpec(memory_space=pltpu.HBM)
    bf, f32 = jnp.bfloat16, jnp.float32
    return pl.pallas_call(
        attention_kernel,
        out_shape=(
            jax.ShapeDtypeStruct(q_mine.shape, f32),
            jax.ShapeDtypeStruct(q_mine.shape, bf),
            jax.ShapeDtypeStruct(kv.shape, bf),
        ),
        in_specs=[smem] + [hbm] * 5 + [vmem],
        out_specs=(vmem, vmem, hbm),
        scratch_shapes=[
            pltpu.VMEM((4, *q_mine.shape), bf),
            pltpu.VMEM((n_blocks, KEY_BLOCK, kv.shape[1]), bf),
            pltpu.VMEM((KVH, KEY_BLOCK, DH), f32),
            pltpu.VMEM((KVH, KEY_BLOCK, DH), f32),
            pltpu.VMEM((n_blocks, KEY_BLOCK, kv.shape[1]), bf),
            pltpu.VMEM((count, GROUP * HALF, DH), bf),
            pltpu.VMEM((count, GROUP * HALF, DH), bf),
            pltpu.VMEM((count, DH, GROUP * HALF), bf),
            pltpu.VMEM((count, DH, GROUP * HALF), bf),
            pltpu.VMEM((count, DH, GROUP * HALF), f32),
            pltpu.SemaphoreType.DMA((4,)),
            pltpu.SemaphoreType.DMA((n_slots,)),
            pltpu.SemaphoreType.DMA((n_slots,)),
        ],
        compiler_params=pltpu.CompilerParams(vmem_limit_bytes=52 * 1024 * 1024),
    )(table, kv, q_mine, g_mine, q_other, g_other, stats)


def from_everyone(shard, axis):
    count = lax.axis_size(axis)
    return lax.all_to_all(
        jnp.broadcast_to(shard[None], (count, *shard.shape)), axis, 0, 0, tiled=True
    )


def swapped(block):
    return lax.ppermute(block, "ctx_1", PAIR)


def stat_rows(stats):
    tall = stats.reshape(ROWS // HALF, HALF, KVH, GROUP)
    return jnp.transpose(tall, (2, 0, 3, 1)).reshape(KVH, ROWS // HALF, GROUP * HALF)


def span_tables(span_ids):
    me_x = lax.axis_index("ctx_1")
    places = span_ids.reshape(lax.axis_size("ctx_0"), 2, ROWS // HALF)
    key_spans = lax.dynamic_index_in_dim(places, me_x, 1, keepdims=False).reshape(-1)
    here = lax.dynamic_index_in_dim(places, lax.axis_index("ctx_0"), 0, keepdims=False)
    own = lax.dynamic_index_in_dim(here, me_x, 0, keepdims=False)
    other = lax.dynamic_index_in_dim(here, 1 - me_x, 0, keepdims=False)
    spans = jnp.concatenate([own, other])
    count = key_spans.shape[0]
    slots = jnp.arange(count, dtype=jnp.int32)
    rank = jnp.sum((key_spans[None, :] < key_spans[:, None]).astype(jnp.int32), axis=1)
    at_rank = rank[None, :] == slots[:, None]
    slot_of = jnp.sum(jnp.where(at_rank, slots[None, :], 0), axis=1)
    pos_of = jnp.sum(jnp.where(at_rank, key_spans[None, :], 0), axis=1)
    less = jnp.sum((key_spans[None, :] < spans[:, None]).astype(jnp.int32), axis=1)
    seen = jnp.sum((key_spans[None, :] <= spans[:, None]).astype(jnp.int32), axis=1)
    return jnp.concatenate([slot_of, pos_of, spans, less, seen])


def per_device(
    span_ids,
    hidden_in,
    queries,
    keys_in,
    values_in,
    attn_out,
    out_grad,
    log_norm,
    adapter,
    moment_first,
    moment_second,
):
    f32, low = jnp.float32, jnp.bfloat16
    z_count = lax.axis_size("ctx_0")
    dp_count = lax.axis_size("dp")
    width = adapter.shape[1]
    query_rows, grad_rows, input_rows = queries[0], out_grad[0], hidden_in[0]

    kv_rows = jnp.concatenate([keys_in[0], values_in[0]], axis=1)
    kv_all = lax.all_gather(kv_rows, "ctx_0", axis=0, tiled=True)

    query_other = swapped(query_rows)
    grad_other = swapped(grad_rows)
    products = grad_rows.astype(f32) * attn_out[0].astype(f32)
    delta = jnp.sum(products.reshape(ROWS, H, DH), axis=-1)
    own_stats = jnp.stack([stat_rows(log_norm[0]), stat_rows(delta)])
    stats = jnp.concatenate([own_stats, swapped(own_stats)], axis=2)
    stats = stats.reshape(2, 2 * KVH * ROWS // HALF, GROUP * HALF)
    table = span_tables(span_ids[0])

    adapter_low = from_everyone(adapter.astype(low), "dp")
    adapter_low = jnp.transpose(adapter_low, (1, 0, 2)).reshape(adapter.shape[0], dp_count * width)
    mixed_down = lax.dot_general(
        adapter_low[:, :D], input_rows, (((1,), (1,)), ((), ())), preferred_element_type=f32
    ).astype(low)
    mixed_down = from_everyone(mixed_down, "ctx_0")
    mixed_down = jnp.transpose(mixed_down, (1, 0, 2)).reshape(adapter.shape[0], z_count * ROWS)

    stats, mixed_down, adapter_low = lax.optimization_barrier((stats, mixed_down, adapter_low))
    query_terms, other_terms, kv_part = attention_terms(
        table, kv_all, query_rows, grad_rows, query_other, grad_other, stats
    )
    kv_low = lax.psum_scatter(kv_part, "ctx_0", scatter_dimension=0, tiled=True)

    query_grad = (query_terms + swapped(other_terms).astype(f32)).astype(low)

    up_terms = lax.dot_general(
        adapter_low[:, D:], kv_part, (((1,), (1,)), ((), ())), preferred_element_type=f32
    )
    up_terms = jnp.transpose(up_terms.reshape(adapter.shape[0], z_count, ROWS), (1, 0, 2))
    mixed_up = lax.all_to_all(up_terms, "ctx_0", 0, 0, tiled=True).sum(axis=0).astype(low)
    grad_up = jnp.dot(mixed_down, kv_part, preferred_element_type=f32)
    grad_down = jnp.dot(mixed_up, input_rows, preferred_element_type=f32)
    grad_partial = jnp.concatenate([grad_down, grad_up], axis=1).astype(low)
    pieces = jnp.transpose(grad_partial.reshape(adapter.shape[0], dp_count, width), (1, 0, 2))
    pieces = jnp.broadcast_to(pieces[:, None], (dp_count, 2, *adapter.shape))
    pieces = pieces.reshape(2 * dp_count, *adapter.shape)
    arrived = lax.all_to_all(pieces, ("dp", "ctx_1"), 0, 0, tiled=True)
    grad_shard = arrived.astype(f32).sum(axis=0)
    grad_shard = from_everyone(grad_shard.astype(low), "ctx_0").astype(f32).sum(axis=0)
    squares = from_everyone(jnp.sum(grad_shard * grad_shard), "dp").sum(axis=0)
    clip_factor = jnp.minimum(1.0, 1.0 / jnp.sqrt(squares + 1e-06))
    scaled = grad_shard * clip_factor
    moment_new = 0.9 * moment_first + 0.1 * scaled
    second_new = 0.999 * moment_second + 0.001 * scaled * scaled
    adapter_step = moment_new / BIAS_ONE / (jnp.sqrt(second_new / BIAS_TWO) + 1e-08)
    return (query_grad[None], kv_low[None], adapter_step)


def solution(mesh):
    torus = Mesh(mesh.devices.reshape(mesh.shape["dp"], -1, 2), ("dp", "ctx_0", "ctx_1"))
    placed = (
        P("dp", None),
        P("dp", CTX, None),
        P("dp", CTX, None),
        P("dp", CTX, None),
        P("dp", CTX, None),
        P("dp", CTX, None),
        P("dp", CTX, None),
        P("dp", CTX, None),
        P(None, "dp"),
        P(None, "dp"),
        P(None, "dp"),
    )
    return jax.shard_map(
        per_device,
        mesh=torus,
        in_specs=placed,
        out_specs=(P("dp", CTX, None), P("dp", CTX, None), P(None, "dp")),
        check_vma=False,
    )
```

time: 219 us -> 204 us (0.932)
  local copies, waits for them, and re-layouts: 20.4 us -> 5.72 us
  waiting for transfers between devices: 72.2 us -> 80.4 us
  Pallas kernels: 26.2 us -> 21.5 us
  other arithmetic: 10.5 us -> 8.28 us
    unnamed x35 -> x17, local copies, waits for them, and re-layouts: 14.7 us -> 0.74 us
    all_to_all x4, waiting for transfers between devices: 21 us -> 27.1 us  [from_everyone(): lax.all_to_all(jnp.broadcast_to(shard[None], (count, *shard.shape)), axis...]
    pallas_call x2 -> x1, Pallas kernels: 26.2 us -> 21.5 us  [attention_terms(): pl.pallas_call(attention_kernel, out_shape=(jax.ShapeDtypeStruct(q_mine.s...]
    all_gather x1, waiting for transfers between devices: 30.4 us -> 32.8 us  [per_device(): kv_all = lax.all_gather(kv_rows, 'ctx_0', axis=0, tiled=True)]
  transfers between devices with their start and end apart: 11 -> 11, of which waited for: 6 -> 6; matrix products, arithmetic and copies ran while one was open for 11% -> 10% of each run, Pallas kernels for 0% -> 0%
where the time goes in v2:
time: 204 us; the launch traced here: 203 us
  waiting for transfers between devices  80.4 us (39%)
  starting transfers between devices  49.4 us (24%)
  Pallas kernels  21.5 us (11%)
  between operations  15 us (7%)
  blocking collectives  14.7 us (7%)
  other arithmetic  8.28 us (4%)
  matrix products  7.52 us (4%)
  local copies, waits for them, and re-layouts  5.72 us (3%)
    all_gather x1, waiting for transfers between devices, per_device(): kv_all = lax.all_gather(kv_rows, 'ctx_0', axis=0, tiled=True)  32.8 us
    all_to_all x4, waiting for transfers between devices, from_everyone(): lax.all_to_all(jnp.broadcast_to(shard[None], (count, *shard.shape)), axis...  27.1 us
    all_to_all x4, starting transfers between devices, from_everyone(): lax.all_to_all(jnp.broadcast_to(shard[None], (count, *shard.shape)), axis...  25.2 us
    pallas_call x1, Pallas kernels, attention_terms(): pl.pallas_call(attention_kernel, out_shape=(jax.ShapeDtypeStruct(q_mine.s...  21.5 us
    ppermute x4, starting transfers between devices, swapped(): return lax.ppermute(block, 'ctx_1', PAIR)  17.9 us
    all_to_all x1, blocking collectives, per_device(): arrived = lax.all_to_all(pieces, ('dp', 'ctx_1'), 0, 0, tiled=True)  14.7 us
    reduce_scatter x1, waiting for transfers between devices, per_device(): kv_low = lax.psum_scatter(kv_part, 'ctx_0', scatter_dimension=0, tiled=True)  10.4 us
    all_to_all x1, waiting for transfers between devices, per_device(): lax.all_to_all(up_terms, 'ctx_0', 0, 0, tiled=True).sum(axis=0).astype(low)  10.1 us
  transfers between devices with their start and end apart: 11, of which 6 were waited for; matrix products, arithmetic and copies ran while one was open for 10% of the time, Pallas kernels for 0%

profile of v2, /device:TPU:6, one launch (start us, length us, event | category | flops | bytes accessed | tf_op | source)
XLA Modules:
  0.0 202.5 jit_solution(2515572136993227774)
XLA Ops:
  7.3 1.8 pad_maximum_fusion
  10.5 5.9 %all-to-all-start = ((bf16[16,8,320]{2,1,0:T(8,128)(2,1)}), bf16[16,8,320]{2,1,0:T(8,128)(2,1)S(1)}, u32[]{:S(2)}, u32[]{:S(2)}) async-start(bf16[16,8,320]{2,1,0:T(8,128)(2,1)} %broadcast_in_dim.32), calls=%async_computation | async-start | bytes 196608 | tf_op jit(solution)/shard_map/all_to_all | solution.py:218
  16.4 6.6 %collective-permute-start = (bf16[128,2048]{1,0:T(8,128)(2,1)}, bf16[128,2048]{1,0:T(8,128)(2,1)}, u32[]{:S(2)}, u32[]{:S(2)}) collective-permute-start(bf16[128,2048]{1,0:T(8,128)(2,1)} %bitcast.44), channel_id=1, source_target_pairs={{0,1},{1,0},{2,3},{3,2},{4,5},{5,4},{6,7},{7,6},{8,9},{9,8},{10,11... | collective-permute-start | bytes 1572872 | tf_op jit(solution)/shard_map/ppermute | solution.py:224
  23.0 1.9 collective-permute-start.1
  24.9 0.8 reshape_squeeze.7
  25.8 1.3 multiply_bitcast_fusion
  28.0 5.4 %collective-permute-start.2 = (f32[2,4,2,256]{3,2,1,0:T(2,128)S(1)}, f32[2,4,2,256]{3,2,1,0:T(2,128)S(1)}, u32[]{:S(2)}, u32[]{:S(2)}) collective-permute-start(f32[2,4,2,256]{3,2,1,0:T(2,128)S(1)} %constant_dynamic-update-slice_fusion), channel_id=1, source_target_pairs={{0,1},{1,0},{2,3},{3,2},{4,5},{5,4},{6,7},{7,6},{8,9},{9,8},{10,11... | collective-permute-start | bytes 49160 | tf_op jit(solution)/shard_map/ppermute | solution.py:224
  36.5 11.9 %all-to-all-start.1 = ((bf16[16,8,128]{2,1,0:T(8,128)(2,1)}), bf16[16,8,128]{2,1,0:T(8,128)(2,1)S(1)}, u32[]{:S(2)}, u32[]{:S(2)}) async-start(bf16[16,8,128]{2,1,0:T(8,128)(2,1)} %broadcast_in_dim.33), calls=%async_computation.1 | async-start | bytes 65536 | tf_op jit(solution)/shard_map/all_to_all | solution.py:218
  48.7 12.6 %all-to-all-done.1 = bf16[16,8,128]{2,1,0:T(8,128)(2,1)S(1)} async-done(((bf16[16,8,128]{2,1,0:T(8,128)(2,1)}), bf16[16,8,128]{2,1,0:T(8,128)(2,1)S(1)}, u32[]{:S(2)}, u32[]{:S(2)}) %all-to-all-start.1) | async-done | bytes 32800 | tf_op jit(solution)/shard_map/all_to_all | solution.py:218
  61.3 32.8 %all-gather.2.cloned.1.call-done.kv_hbm = bf16[2048,1024]{1,0:T(8,128)(2,1)} async-done(((bf16[128,1024]{1,0:T(8,128)(2,1)}), bf16[2048,1024]{1,0:T(8,128)(2,1)}) %all-gather.2.cloned.1.call-update) | async-done | bytes 4194320 | tf_op jit(solution)/shard_map/all_gather | solution.py:271
  94.1 21.5 %shard_map.130 = (f32[128,2048]{1,0:T(8,128)}, bf16[128,2048]{1,0:T(8,128)(2,1)S(1)}, bf16[2048,1024]{1,0:T(8,128)(2,1)}) custom-call(s32[76]{0:T(128)S(1)} %concatenate.18.table_ref, bf16[2048,1024]{1,0:T(8,128)(2,1)} %all-gather.2.cloned.1.call-done.kv_hbm, bf16[128,2048]{1,0:T(8,128)(2,1)S(1)} %bitcast.45, bf16[128,2048]{1,0:T(8,128)(2,1)S(1)} %bitcast.43, ...), custom_call_target="tpu_custom_call" | custom-call | tf_op jit(solution)/shard_map/pallas_call | solution.py:188
  115.6 4.0 %convolution_bitcast_fusion = f32[16,8,128]{2,1,0:T(8,128)} fusion(bf16[2048,1024]{1,0:T(8,128)(2,1)} %get-tuple-element.12, bf16[8,5120]{1,0:T(8,128)(2,1)S(1)} %reshape.52), kind=kOutput, calls=%fused_computation.1 | convolution fusion | flops 33554432 | bytes 4276224 | tf_op jit(solution)/shard_map/dot_general | solution.py:298
  119.6 6.2 %all-to-all-start.2 = ((f32[16,8,128]{2,1,0:T(8,128)}), f32[16,8,128]{2,1,0:T(8,128)S(1)}, u32[]{:S(2)}, u32[]{:S(2)}) async-start(f32[16,8,128]{2,1,0:T(8,128)} %convolution_bitcast_fusion), calls=%async_computation.3 | async-start | bytes 131072 | tf_op jit(solution)/shard_map/all_to_all | solution.py:302
  125.9 2.9 %convolution_convert_fusion.1 = bf16[8,1024]{1,0:T(8,128)(2,1)S(1)} fusion(bf16[8,2048]{1,0:T(8,128)(2,1)S(1)} %bitcast.50, bf16[2048,1024]{1,0:T(8,128)(2,1)} %get-tuple-element.12), kind=kOutput, calls=%fused_computation.2 | convolution fusion | flops 33562624 | bytes 4243456 | tf_op jit(solution)/shard_map/dot_general | solution.py:303
  128.8 10.1 %all-to-all-done.2 = f32[16,8,128]{2,1,0:T(8,128)S(1)} async-done(((f32[16,8,128]{2,1,0:T(8,128)}), f32[16,8,128]{2,1,0:T(8,128)S(1)}, u32[]{:S(2)}, u32[]{:S(2)}) %all-to-all-start.2) | async-done | bytes 65568 | tf_op jit(solution)/shard_map/all_to_all | solution.py:302
  139.3 14.7 %all_to_all.31 = bf16[32,8,320]{2,1,0:T(8,128)(2,1)S(1)} all-to-all(bf16[32,8,320]{2,1,0:T(8,128)(2,1)S(1)} %bitcast.47), channel_id=1, replica_groups=mesh['dp'=16,'ctx_0'=16,'ctx_1'=2] {'dp','ctx_1'}, dimensions={0} | all-to-all | bytes 327680 | tf_op jit(solution)/shard_map/all_to_all | solution.py:309
  154.7 3.5 %all-to-all-start.4 = ((bf16[16,8,320]{2,1,0:T(8,128)(2,1)}), bf16[16,8,320]{2,1,0:T(8,128)(2,1)S(1)}, u32[]{:S(2)}, u32[]{:S(2)}) async-start(bf16[16,8,320]{2,1,0:T(8,128)(2,1)} %broadcast_in_dim.64), calls=%async_computation.5 | async-start | bytes 196608 | tf_op jit(solution)/shard_map/all_to_all | solution.py:218
  158.2 4.0 %collective-permute-start.3 = (bf16[128,2048]{1,0:T(8,128)(2,1)S(1)}, bf16[128,2048]{1,0:T(8,128)(2,1)S(1)}, u32[]{:S(2)}, u32[]{:S(2)}) collective-permute-start(bf16[128,2048]{1,0:T(8,128)(2,1)S(1)} %get-tuple-element.11), channel_id=1, source_target_pairs={{0,1},{1,0},{2,3},{3,2},{4,5},{5,4},{6,7},{7,6},{8,9},{9,8},{10,11... | collective-permute-start | bytes 1572872 | tf_op jit(solution)/shard_map/ppermute | solution.py:224
  162.2 10.8 %all-to-all-done.4 = bf16[16,8,320]{2,1,0:T(8,128)(2,1)S(1)} async-done(((bf16[16,8,320]{2,1,0:T(8,128)(2,1)}), bf16[16,8,320]{2,1,0:T(8,128)(2,1)S(1)}, u32[]{:S(2)}, u32[]{:S(2)}) %all-to-all-start.4) | async-done | bytes 81952 | tf_op jit(solution)/shard_map/all_to_all | solution.py:218
  173.6 1.2 broadcast_in_dim.65
  174.8 3.9 %all-to-all-start.5 = ((f32[16,1,1]{2,1,0:T(1,128)}), f32[16,1,1]{2,1,0:T(1,128)S(1)}, u32[]{:S(2)}, u32[]{:S(2)}) async-start(f32[16,1,1]{2,1,0:T(1,128)} %broadcast_in_dim.65), calls=%async_computation.6 | async-start | bytes 16384 | tf_op jit(solution)/shard_map/all_to_all | solution.py:218
  178.7 0.9 fusion.2
  179.6 3.8 %all-to-all-done.5 = f32[16,1,1]{2,1,0:T(1,128)S(1)} async-done(((f32[16,1,1]{2,1,0:T(1,128)}), f32[16,1,1]{2,1,0:T(1,128)S(1)}, u32[]{:S(2)}, u32[]{:S(2)}) %all-to-all-start.5) | async-done | bytes 96 | tf_op jit(solution)/shard_map/all_to_all | solution.py:218
  185.3 10.4 %reduce-scatter.2.cloned.1.call-done = bf16[128,1024]{1,0:T(8,128)(2,1)} async-done(((bf16[2048,1024]{1,0:T(8,128)(2,1)}), bf16[128,1024]{1,0:T(8,128)(2,1)}) %reduce-scatter.2.cloned.1.call-update) | async-done | bytes 262160 | tf_op jit(solution)/shard_map/reduce_scatter | solution.py:294
  (64 shorter events, 8.7 us)
Async XLA Ops:
  7.2 28.3 %copy-start = (bf16[1,128,4096]{2,1,0:T(8,128)(2,1)S(1)}, bf16[1,128,4096]{2,1,0:T(8,128)(2,1)}, u32[]{:S(2)}) copy-start(bf16[1,128,4096]{2,1,0:T(8,128)(2,1)} %param.12) | copy-start | bytes 3145732
  7.2 26.7 %copy-start.6 = (s32[1,64]{1,0:T(1,128)S(1)}, s32[1,64]{1,0:T(1,128)}, u32[]{:S(2)}) copy-start(s32[1,64]{1,0:T(1,128)} %param.11) | copy-start | bytes 772
  7.2 86.9 %all-gather.2.cloned.1.call-start = ((), (), s32[]{:S(2)}) async-start(), calls=%async_computation.7 | async-start | bytes 4456448 | tf_op jit(solution)/shard_map/all_gather | solution.py:271
  7.2 86.9 %copy-start.1 = (bf16[1,128,2048]{2,1,0:T(8,128)(2,1)S(1)}, bf16[1,128,2048]{2,1,0:T(8,128)(2,1)}, u32[]{:S(2)}) copy-start(bf16[1,128,2048]{2,1,0:T(8,128)(2,1)} %param.17) | copy-start | bytes 1572868
  7.2 86.9 %copy-start.2 = (bf16[1,128,2048]{2,1,0:T(8,128)(2,1)S(1)}, bf16[1,128,2048]{2,1,0:T(8,128)(2,1)}, u32[]{:S(2)}) copy-start(bf16[1,128,2048]{2,1,0:T(8,128)(2,1)} %param.13) | copy-start | bytes 1572868
  10.5 24.8 %all-to-all-start = ((bf16[16,8,320]{2,1,0:T(8,128)(2,1)}), bf16[16,8,320]{2,1,0:T(8,128)(2,1)S(1)}, u32[]{:S(2)}, u32[]{:S(2)}) async-start(bf16[16,8,320]{2,1,0:T(8,128)(2,1)} %broadcast_in_dim.32), calls=%async_computation | async-start | bytes 196608 | tf_op jit(solution)/shard_map/all_to_all | solution.py:218
  16.4 44.9 %collective-permute-start = (bf16[128,2048]{1,0:T(8,128)(2,1)}, bf16[128,2048]{1,0:T(8,128)(2,1)}, u32[]{:S(2)}, u32[]{:S(2)}) collective-permute-start(bf16[128,2048]{1,0:T(8,128)(2,1)} %bitcast.44), channel_id=1, source_target_pairs={{0,1},{1,0},{2,3},{3,2},{4,5},{5,4},{6,7},{7,6},{8,9},{9,8},{10,11... | collective-permute-start | bytes 1572872 | tf_op jit(solution)/shard_map/ppermute | solution.py:224
  23.0 38.3 %collective-permute-start.1 = (bf16[128,2048]{1,0:T(8,128)(2,1)}, bf16[128,2048]{1,0:T(8,128)(2,1)}, u32[]{:S(2)}, u32[]{:S(2)}) collective-permute-start(bf16[128,2048]{1,0:T(8,128)(2,1)} %bitcast.42), channel_id=1, source_target_pairs={{0,1},{1,0},{2,3},{3,2},{4,5},{5,4},{6,7},{7,6},{8,9},{9,8},{10,11... | collective-permute-start | bytes 1572872 | tf_op jit(solution)/shard_map/ppermute | solution.py:224
  28.0 20.7 %collective-permute-start.2 = (f32[2,4,2,256]{3,2,1,0:T(2,128)S(1)}, f32[2,4,2,256]{3,2,1,0:T(2,128)S(1)}, u32[]{:S(2)}, u32[]{:S(2)}) collective-permute-start(f32[2,4,2,256]{3,2,1,0:T(2,128)S(1)} %constant_dynamic-update-slice_fusion), channel_id=1, source_target_pairs={{0,1},{1,0},{2,3},{3,2},{4,5},{5,4},{6,7},{7,6},{8,9},{9,8},{10,11... | collective-permute-start | bytes 49160 | tf_op jit(solution)/shard_map/ppermute | solution.py:224
  36.5 24.8 %all-to-all-start.1 = ((bf16[16,8,128]{2,1,0:T(8,128)(2,1)}), bf16[16,8,128]{2,1,0:T(8,128)(2,1)S(1)}, u32[]{:S(2)}, u32[]{:S(2)}) async-start(bf16[16,8,128]{2,1,0:T(8,128)(2,1)} %broadcast_in_dim.33), calls=%async_computation.1 | async-start | bytes 65536 | tf_op jit(solution)/shard_map/all_to_all | solution.py:218
  48.4 147.3 %reduce-scatter.2.cloned.1.call-start = ((), (), s32[]{:S(2)}) async-start(), calls=%async_computation.8 | async-start | bytes 4456448 | tf_op jit(solution)/shard_map/reduce_scatter | solution.py:294
  119.6 59.1 %copy-start.3 = (f32[128,2048]{1,0:T(8,128)S(1)}, f32[128,2048]{1,0:T(8,128)}, u32[]{:S(2)}) copy-start(f32[128,2048]{1,0:T(8,128)} %get-tuple-element.10) | copy-start | bytes 3145732
  119.6 19.2 %all-to-all-start.2 = ((f32[16,8,128]{2,1,0:T(8,128)}), f32[16,8,128]{2,1,0:T(8,128)S(1)}, u32[]{:S(2)}, u32[]{:S(2)}) async-start(f32[16,8,128]{2,1,0:T(8,128)} %convolution_bitcast_fusion), calls=%async_computation.3 | async-start | bytes 131072 | tf_op jit(solution)/shard_map/all_to_all | solution.py:302
  125.8 58.8 %copy-start.4 = (f32[8,320]{1,0:T(8,128)S(1)}, f32[8,320]{1,0:T(8,128)}, u32[]{:S(2)}) copy-start(f32[8,320]{1,0:T(8,128)} %param.21) | copy-start | bytes 30724
  125.8 58.8 %copy-start.5 = (f32[8,320]{1,0:T(8,128)S(1)}, f32[8,320]{1,0:T(8,128)}, u32[]{:S(2)}) copy-start(f32[8,320]{1,0:T(8,128)} %param.20) | copy-start | bytes 30724
  154.7 18.3 %all-to-all-start.4 = ((bf16[16,8,320]{2,1,0:T(8,128)(2,1)}), bf16[16,8,320]{2,1,0:T(8,128)(2,1)S(1)}, u32[]{:S(2)}, u32[]{:S(2)}) async-start(bf16[16,8,320]{2,1,0:T(8,128)(2,1)} %broadcast_in_dim.64), calls=%async_computation.5 | async-start | bytes 196608 | tf_op jit(solution)/shard_map/all_to_all | solution.py:218
  158.2 20.5 %collective-permute-start.3 = (bf16[128,2048]{1,0:T(8,128)(2,1)S(1)}, bf16[128,2048]{1,0:T(8,128)(2,1)S(1)}, u32[]{:S(2)}, u32[]{:S(2)}) collective-permute-start(bf16[128,2048]{1,0:T(8,128)(2,1)S(1)} %get-tuple-element.11), channel_id=1, source_target_pairs={{0,1},{1,0},{2,3},{3,2},{4,5},{5,4},{6,7},{7,6},{8,9},{9,8},{10,11... | collective-permute-start | bytes 1572872 | tf_op jit(solution)/shard_map/ppermute | solution.py:224
  174.8 8.5 %all-to-all-start.5 = ((f32[16,1,1]{2,1,0:T(1,128)}), f32[16,1,1]{2,1,0:T(1,128)S(1)}, u32[]{:S(2)}, u32[]{:S(2)}) async-start(f32[16,1,1]{2,1,0:T(1,128)} %broadcast_in_dim.65), calls=%async_computation.6 | async-start | bytes 16384 | tf_op jit(solution)/shard_map/all_to_all | solution.py:218
Sparse Core Ops, SparseCore 0:
  10.7 83.4 all-gather.1
  115.7 79.8 reduce-scatter.1

commit v3 on v2

--- a/solution.py
+++ b/solution.py
@@ -57,11 +57,15 @@
             dkv_s.at[rank // per_block, pl.ds(place, HALF), :], dkv_hbm.at[pl.ds(row, HALF), :], out_sem.at[rank]
         )
 
-    def start_in(rank, carry):
-        span_in(rank).start()
+    def block_at(turn):
+        return jnp.where(turn == 0, 0, n_blocks - turn)
+
+    def start_in(turn, carry):
+        for i in range(per_block):
+            span_in(block_at(turn) * per_block + i).start()
         return carry
 
-    lax.fori_loop(0, pos_at, start_in, 0)
+    lax.fori_loop(0, n_blocks, start_in, 0)
     for copy in raw_copies:
         copy.wait()
 
@@ -88,7 +92,7 @@
     def value_cols(j):
         return slice(value_at + j * DH, value_at + (j + 1) * DH)
 
-    def heads(b, s, masked):
+    def heads(b, s, masked, rows=KEY_BLOCK):
         if masked:
             lane = lax.broadcasted_iota(jnp.int32, (HALF, n_rows), 1)
             line = lax.broadcasted_iota(jnp.int32, (HALF, n_rows), 0)
@@ -96,14 +100,14 @@
             visible = jnp.concatenate(
                 [
                     ahead <= (table_ref[span_at + s] - table_ref[pos_at + b * per_block + i]) * HALF
-                    for i in range(per_block)
+                    for i in range(rows // HALF)
                 ],
                 axis=0,
             )
         def front(j):
             n = j * n_spans + s
-            scores = jnp.dot(kv_s[b, :, key_cols(j)], qt_s[n], preferred_element_type=jnp.float32)
-            d_weights = jnp.dot(kv_s[b, :, value_cols(j)], gt_s[n], preferred_element_type=jnp.float32)
+            scores = jnp.dot(kv_s[b, :rows, key_cols(j)], qt_s[n], preferred_element_type=jnp.float32)
+            d_weights = jnp.dot(kv_s[b, :rows, value_cols(j)], gt_s[n], preferred_element_type=jnp.float32)
             return scores, d_weights
 
         def middle(j, scores, d_weights):
@@ -116,10 +120,10 @@
 
         def back(j, weights_low, d_scores):
             n = j * n_spans + s
-            dv_s[j] += jnp.dot(weights_low, g_s[n], preferred_element_type=jnp.float32)
-            dk_s[j] += jnp.dot(d_scores, q_s[n], preferred_element_type=jnp.float32)
+            dv_s[j, :rows] += jnp.dot(weights_low, g_s[n], preferred_element_type=jnp.float32)
+            dk_s[j, :rows] += jnp.dot(d_scores, q_s[n], preferred_element_type=jnp.float32)
             dqt_s[n] += lax.dot_general(
-                kv_s[b, :, key_cols(j)], d_scores, (((0,), (0,)), ((), ())), preferred_element_type=jnp.float32
+                kv_s[b, :rows, key_cols(j)], d_scores, (((0,), (0,)), ((), ())), preferred_element_type=jnp.float32
             )
 
         fronts = front(0)
@@ -129,7 +133,8 @@
                 fronts = front(j + 1)
             back(j, *middles)
 
-    def block(b, carry):
+    def block(turn, carry):
+        b = block_at(turn)
         for i in range(per_block):
             span_in(b * per_block + i).wait()
         for j in range(KVH):
@@ -143,9 +148,15 @@
             def _():
                 heads(b, s, False)
 
-            @pl.when(jnp.logical_and(jnp.logical_not(whole), table_ref[seen_at + s] > b * per_block))
+            seen = table_ref[seen_at + s] - b * per_block
+
+            @pl.when(jnp.logical_and(jnp.logical_not(whole), seen > per_block // 2))
             def _():
                 heads(b, s, True)
+
+            @pl.when(jnp.logical_and(seen > 0, seen <= per_block // 2))
+            def _():
+                heads(b, s, True, KEY_BLOCK // 2)
 
             return c
 

time: 204 us -> 204 us (level)
  no operation moved by 1% of the time
where the time goes in v3:
time: 204 us; the launch traced here: 203 us
  waiting for transfers between devices  80.4 us (39%)
  starting transfers between devices  50.2 us (25%)
  Pallas kernels  21.4 us (10%)
  between operations  15 us (7%)
  blocking collectives  14.1 us (7%)
  other arithmetic  8.28 us (4%)
  matrix products  7.66 us (4%)
  local copies, waits for them, and re-layouts  5.72 us (3%)
    all_gather x1, waiting for transfers between devices, per_device(): kv_all = lax.all_gather(kv_rows, 'ctx_0', axis=0, tiled=True)  32.8 us
    all_to_all x4, waiting for transfers between devices, from_everyone(): lax.all_to_all(jnp.broadcast_to(shard[None], (count, *shard.shape)), axis...  27 us
    all_to_all x4, starting transfers between devices, from_everyone(): lax.all_to_all(jnp.broadcast_to(shard[None], (count, *shard.shape)), axis...  25.5 us
    pallas_call x1, Pallas kernels, attention_terms(): pl.pallas_call(attention_kernel, out_shape=(jax.ShapeDtypeStruct(q_mine.s...  21.4 us
    ppermute x4, starting transfers between devices, swapped(): return lax.ppermute(block, 'ctx_1', PAIR)  17.9 us
    all_to_all x1, blocking collectives, per_device(): arrived = lax.all_to_all(pieces, ('dp', 'ctx_1'), 0, 0, tiled=True)  14.1 us
    reduce_scatter x1, waiting for transfers between devices, per_device(): kv_low = lax.psum_scatter(kv_part, 'ctx_0', scatter_dimension=0, tiled=True)  10.5 us
    all_to_all x1, waiting for transfers between devices, per_device(): lax.all_to_all(up_terms, 'ctx_0', 0, 0, tiled=True).sum(axis=0).astype(low)  10 us
  transfers between devices with their start and end apart: 11, of which 6 were waited for; matrix products, arithmetic and copies ran while one was open for 10% of the time, Pallas kernels for 0%

profile of v3, /device:TPU:6, one launch (start us, length us, event | category | flops | bytes accessed | tf_op | source)
XLA Modules:
  0.0 202.9 jit_solution(18214960466656830504)
XLA Ops:
  7.3 1.8 pad_maximum_fusion
  10.5 5.9 %all-to-all-start = ((bf16[16,8,320]{2,1,0:T(8,128)(2,1)}), bf16[16,8,320]{2,1,0:T(8,128)(2,1)S(1)}, u32[]{:S(2)}, u32[]{:S(2)}) async-start(bf16[16,8,320]{2,1,0:T(8,128)(2,1)} %broadcast_in_dim.32), calls=%async_computation | async-start | bytes 196608 | tf_op jit(solution)/shard_map/all_to_all | solution.py:229
  16.4 6.6 %collective-permute-start = (bf16[128,2048]{1,0:T(8,128)(2,1)}, bf16[128,2048]{1,0:T(8,128)(2,1)}, u32[]{:S(2)}, u32[]{:S(2)}) collective-permute-start(bf16[128,2048]{1,0:T(8,128)(2,1)} %bitcast.44), channel_id=1, source_target_pairs={{0,1},{1,0},{2,3},{3,2},{4,5},{5,4},{6,7},{7,6},{8,9},{9,8},{10,11... | collective-permute-start | bytes 1572872 | tf_op jit(solution)/shard_map/ppermute | solution.py:235
  23.0 1.9 collective-permute-start.1
  24.9 0.8 reshape_squeeze.7
  25.8 1.3 multiply_bitcast_fusion
  28.0 5.4 %collective-permute-start.2 = (f32[2,4,2,256]{3,2,1,0:T(2,128)S(1)}, f32[2,4,2,256]{3,2,1,0:T(2,128)S(1)}, u32[]{:S(2)}, u32[]{:S(2)}) collective-permute-start(f32[2,4,2,256]{3,2,1,0:T(2,128)S(1)} %constant_dynamic-update-slice_fusion), channel_id=1, source_target_pairs={{0,1},{1,0},{2,3},{3,2},{4,5},{5,4},{6,7},{7,6},{8,9},{9,8},{10,11... | collective-permute-start | bytes 49160 | tf_op jit(solution)/shard_map/ppermute | solution.py:235
  36.5 11.9 %all-to-all-start.1 = ((bf16[16,8,128]{2,1,0:T(8,128)(2,1)}), bf16[16,8,128]{2,1,0:T(8,128)(2,1)S(1)}, u32[]{:S(2)}, u32[]{:S(2)}) async-start(bf16[16,8,128]{2,1,0:T(8,128)(2,1)} %broadcast_in_dim.33), calls=%async_computation.1 | async-start | bytes 65536 | tf_op jit(solution)/shard_map/all_to_all | solution.py:229
  48.7 12.6 %all-to-all-done.1 = bf16[16,8,128]{2,1,0:T(8,128)(2,1)S(1)} async-done(((bf16[16,8,128]{2,1,0:T(8,128)(2,1)}), bf16[16,8,128]{2,1,0:T(8,128)(2,1)S(1)}, u32[]{:S(2)}, u32[]{:S(2)}) %all-to-all-start.1) | async-done | bytes 32800 | tf_op jit(solution)/shard_map/all_to_all | solution.py:229
  61.3 32.8 %all-gather.2.cloned.1.call-done.kv_hbm = bf16[2048,1024]{1,0:T(8,128)(2,1)} async-done(((bf16[128,1024]{1,0:T(8,128)(2,1)}), bf16[2048,1024]{1,0:T(8,128)(2,1)}) %all-gather.2.cloned.1.call-update) | async-done | bytes 4194320 | tf_op jit(solution)/shard_map/all_gather | solution.py:282
  94.1 21.4 %shard_map.130 = (f32[128,2048]{1,0:T(8,128)}, bf16[128,2048]{1,0:T(8,128)(2,1)S(1)}, bf16[2048,1024]{1,0:T(8,128)(2,1)}) custom-call(s32[76]{0:T(128)S(1)} %concatenate.18.table_ref, bf16[2048,1024]{1,0:T(8,128)(2,1)} %all-gather.2.cloned.1.call-done.kv_hbm, bf16[128,2048]{1,0:T(8,128)(2,1)S(1)} %bitcast.45, bf16[128,2048]{1,0:T(8,128)(2,1)S(1)} %bitcast.43, ...), custom_call_target="tpu_custom_call" | custom-call | tf_op jit(solution)/shard_map/pallas_call | solution.py:199
  115.6 4.0 %convolution_bitcast_fusion = f32[16,8,128]{2,1,0:T(8,128)} fusion(bf16[2048,1024]{1,0:T(8,128)(2,1)} %get-tuple-element.12, bf16[8,5120]{1,0:T(8,128)(2,1)S(1)} %reshape.52), kind=kOutput, calls=%fused_computation.1 | convolution fusion | flops 33554432 | bytes 4276224 | tf_op jit(solution)/shard_map/dot_general | solution.py:309
  119.6 6.7 %all-to-all-start.2 = ((f32[16,8,128]{2,1,0:T(8,128)}), f32[16,8,128]{2,1,0:T(8,128)S(1)}, u32[]{:S(2)}, u32[]{:S(2)}) async-start(f32[16,8,128]{2,1,0:T(8,128)} %convolution_bitcast_fusion), calls=%async_computation.3 | async-start | bytes 131072 | tf_op jit(solution)/shard_map/all_to_all | solution.py:313
  126.4 3.0 %convolution_convert_fusion.1 = bf16[8,1024]{1,0:T(8,128)(2,1)S(1)} fusion(bf16[8,2048]{1,0:T(8,128)(2,1)S(1)} %bitcast.50, bf16[2048,1024]{1,0:T(8,128)(2,1)} %get-tuple-element.12), kind=kOutput, calls=%fused_computation.2 | convolution fusion | flops 33562624 | bytes 4243456 | tf_op jit(solution)/shard_map/dot_general | solution.py:314
  129.4 10.0 %all-to-all-done.2 = f32[16,8,128]{2,1,0:T(8,128)S(1)} async-done(((f32[16,8,128]{2,1,0:T(8,128)}), f32[16,8,128]{2,1,0:T(8,128)S(1)}, u32[]{:S(2)}, u32[]{:S(2)}) %all-to-all-start.2) | async-done | bytes 65568 | tf_op jit(solution)/shard_map/all_to_all | solution.py:313
  139.9 14.1 %all_to_all.31 = bf16[32,8,320]{2,1,0:T(8,128)(2,1)S(1)} all-to-all(bf16[32,8,320]{2,1,0:T(8,128)(2,1)S(1)} %bitcast.47), channel_id=1, replica_groups=mesh['dp'=16,'ctx_0'=16,'ctx_1'=2] {'dp','ctx_1'}, dimensions={0} | all-to-all | bytes 327680 | tf_op jit(solution)/shard_map/all_to_all | solution.py:320
  154.8 3.5 %all-to-all-start.4 = ((bf16[16,8,320]{2,1,0:T(8,128)(2,1)}), bf16[16,8,320]{2,1,0:T(8,128)(2,1)S(1)}, u32[]{:S(2)}, u32[]{:S(2)}) async-start(bf16[16,8,320]{2,1,0:T(8,128)(2,1)} %broadcast_in_dim.64), calls=%async_computation.5 | async-start | bytes 196608 | tf_op jit(solution)/shard_map/all_to_all | solution.py:229
  158.3 4.0 %collective-permute-start.3 = (bf16[128,2048]{1,0:T(8,128)(2,1)S(1)}, bf16[128,2048]{1,0:T(8,128)(2,1)S(1)}, u32[]{:S(2)}, u32[]{:S(2)}) collective-permute-start(bf16[128,2048]{1,0:T(8,128)(2,1)S(1)} %get-tuple-element.11), channel_id=1, source_target_pairs={{0,1},{1,0},{2,3},{3,2},{4,5},{5,4},{6,7},{7,6},{8,9},{9,8},{10,11... | collective-permute-start | bytes 1572872 | tf_op jit(solution)/shard_map/ppermute | solution.py:235
  162.3 10.7 %all-to-all-done.4 = bf16[16,8,320]{2,1,0:T(8,128)(2,1)S(1)} async-done(((bf16[16,8,320]{2,1,0:T(8,128)(2,1)}), bf16[16,8,320]{2,1,0:T(8,128)(2,1)S(1)}, u32[]{:S(2)}, u32[]{:S(2)}) %all-to-all-start.4) | async-done | bytes 81952 | tf_op jit(solution)/shard_map/all_to_all | solution.py:229
  173.6 1.2 broadcast_in_dim.65
  174.8 4.1 %all-to-all-start.5 = ((f32[16,1,1]{2,1,0:T(1,128)}), f32[16,1,1]{2,1,0:T(1,128)S(1)}, u32[]{:S(2)}, u32[]{:S(2)}) async-start(f32[16,1,1]{2,1,0:T(1,128)} %broadcast_in_dim.65), calls=%async_computation.6 | async-start | bytes 16384 | tf_op jit(solution)/shard_map/all_to_all | solution.py:229
  178.9 0.9 fusion.2
  179.8 3.8 %all-to-all-done.5 = f32[16,1,1]{2,1,0:T(1,128)S(1)} async-done(((f32[16,1,1]{2,1,0:T(1,128)}), f32[16,1,1]{2,1,0:T(1,128)S(1)}, u32[]{:S(2)}, u32[]{:S(2)}) %all-to-all-start.5) | async-done | bytes 96 | tf_op jit(solution)/shard_map/all_to_all | solution.py:229
  185.5 10.5 %reduce-scatter.2.cloned.1.call-done = bf16[128,1024]{1,0:T(8,128)(2,1)} async-done(((bf16[2048,1024]{1,0:T(8,128)(2,1)}), bf16[128,1024]{1,0:T(8,128)(2,1)}) %reduce-scatter.2.cloned.1.call-update) | async-done | bytes 262160 | tf_op jit(solution)/shard_map/reduce_scatter | solution.py:305
  (64 shorter events, 8.7 us)
Async XLA Ops:
  7.2 28.3 %copy-start = (bf16[1,128,4096]{2,1,0:T(8,128)(2,1)S(1)}, bf16[1,128,4096]{2,1,0:T(8,128)(2,1)}, u32[]{:S(2)}) copy-start(bf16[1,128,4096]{2,1,0:T(8,128)(2,1)} %param.12) | copy-start | bytes 3145732
  7.2 26.7 %copy-start.6 = (s32[1,64]{1,0:T(1,128)S(1)}, s32[1,64]{1,0:T(1,128)}, u32[]{:S(2)}) copy-start(s32[1,64]{1,0:T(1,128)} %param.11) | copy-start | bytes 772
  7.2 86.9 %all-gather.2.cloned.1.call-start = ((), (), s32[]{:S(2)}) async-start(), calls=%async_computation.7 | async-start | bytes 4456448 | tf_op jit(solution)/shard_map/all_gather | solution.py:282
  7.2 86.9 %copy-start.1 = (bf16[1,128,2048]{2,1,0:T(8,128)(2,1)S(1)}, bf16[1,128,2048]{2,1,0:T(8,128)(2,1)}, u32[]{:S(2)}) copy-start(bf16[1,128,2048]{2,1,0:T(8,128)(2,1)} %param.17) | copy-start | bytes 1572868
  7.2 86.9 %copy-start.2 = (bf16[1,128,2048]{2,1,0:T(8,128)(2,1)S(1)}, bf16[1,128,2048]{2,1,0:T(8,128)(2,1)}, u32[]{:S(2)}) copy-start(bf16[1,128,2048]{2,1,0:T(8,128)(2,1)} %param.13) | copy-start | bytes 1572868
  10.5 24.8 %all-to-all-start = ((bf16[16,8,320]{2,1,0:T(8,128)(2,1)}), bf16[16,8,320]{2,1,0:T(8,128)(2,1)S(1)}, u32[]{:S(2)}, u32[]{:S(2)}) async-start(bf16[16,8,320]{2,1,0:T(8,128)(2,1)} %broadcast_in_dim.32), calls=%async_computation | async-start | bytes 196608 | tf_op jit(solution)/shard_map/all_to_all | solution.py:229
  16.4 44.9 %collective-permute-start = (bf16[128,2048]{1,0:T(8,128)(2,1)}, bf16[128,2048]{1,0:T(8,128)(2,1)}, u32[]{:S(2)}, u32[]{:S(2)}) collective-permute-start(bf16[128,2048]{1,0:T(8,128)(2,1)} %bitcast.44), channel_id=1, source_target_pairs={{0,1},{1,0},{2,3},{3,2},{4,5},{5,4},{6,7},{7,6},{8,9},{9,8},{10,11... | collective-permute-start | bytes 1572872 | tf_op jit(solution)/shard_map/ppermute | solution.py:235
  23.0 38.3 %collective-permute-start.1 = (bf16[128,2048]{1,0:T(8,128)(2,1)}, bf16[128,2048]{1,0:T(8,128)(2,1)}, u32[]{:S(2)}, u32[]{:S(2)}) collective-permute-start(bf16[128,2048]{1,0:T(8,128)(2,1)} %bitcast.42), channel_id=1, source_target_pairs={{0,1},{1,0},{2,3},{3,2},{4,5},{5,4},{6,7},{7,6},{8,9},{9,8},{10,11... | collective-permute-start | bytes 1572872 | tf_op jit(solution)/shard_map/ppermute | solution.py:235
  28.0 20.7 %collective-permute-start.2 = (f32[2,4,2,256]{3,2,1,0:T(2,128)S(1)}, f32[2,4,2,256]{3,2,1,0:T(2,128)S(1)}, u32[]{:S(2)}, u32[]{:S(2)}) collective-permute-start(f32[2,4,2,256]{3,2,1,0:T(2,128)S(1)} %constant_dynamic-update-slice_fusion), channel_id=1, source_target_pairs={{0,1},{1,0},{2,3},{3,2},{4,5},{5,4},{6,7},{7,6},{8,9},{9,8},{10,11... | collective-permute-start | bytes 49160 | tf_op jit(solution)/shard_map/ppermute | solution.py:235
  36.5 24.8 %all-to-all-start.1 = ((bf16[16,8,128]{2,1,0:T(8,128)(2,1)}), bf16[16,8,128]{2,1,0:T(8,128)(2,1)S(1)}, u32[]{:S(2)}, u32[]{:S(2)}) async-start(bf16[16,8,128]{2,1,0:T(8,128)(2,1)} %broadcast_in_dim.33), calls=%async_computation.1 | async-start | bytes 65536 | tf_op jit(solution)/shard_map/all_to_all | solution.py:229
  48.4 147.6 %reduce-scatter.2.cloned.1.call-start = ((), (), s32[]{:S(2)}) async-start(), calls=%async_computation.8 | async-start | bytes 4456448 | tf_op jit(solution)/shard_map/reduce_scatter | solution.py:305
  119.6 59.3 %copy-start.3 = (f32[128,2048]{1,0:T(8,128)S(1)}, f32[128,2048]{1,0:T(8,128)}, u32[]{:S(2)}) copy-start(f32[128,2048]{1,0:T(8,128)} %get-tuple-element.10) | copy-start | bytes 3145732
  119.6 19.8 %all-to-all-start.2 = ((f32[16,8,128]{2,1,0:T(8,128)}), f32[16,8,128]{2,1,0:T(8,128)S(1)}, u32[]{:S(2)}, u32[]{:S(2)}) async-start(f32[16,8,128]{2,1,0:T(8,128)} %convolution_bitcast_fusion), calls=%async_computation.3 | async-start | bytes 131072 | tf_op jit(solution)/shard_map/all_to_all | solution.py:313
  126.3 58.6 %copy-start.4 = (f32[8,320]{1,0:T(8,128)S(1)}, f32[8,320]{1,0:T(8,128)}, u32[]{:S(2)}) copy-start(f32[8,320]{1,0:T(8,128)} %param.21) | copy-start | bytes 30724
  126.3 58.6 %copy-start.5 = (f32[8,320]{1,0:T(8,128)S(1)}, f32[8,320]{1,0:T(8,128)}, u32[]{:S(2)}) copy-start(f32[8,320]{1,0:T(8,128)} %param.20) | copy-start | bytes 30724
  154.8 18.2 %all-to-all-start.4 = ((bf16[16,8,320]{2,1,0:T(8,128)(2,1)}), bf16[16,8,320]{2,1,0:T(8,128)(2,1)S(1)}, u32[]{:S(2)}, u32[]{:S(2)}) async-start(bf16[16,8,320]{2,1,0:T(8,128)(2,1)} %broadcast_in_dim.64), calls=%async_computation.5 | async-start | bytes 196608 | tf_op jit(solution)/shard_map/all_to_all | solution.py:229
  158.3 20.6 %collective-permute-start.3 = (bf16[128,2048]{1,0:T(8,128)(2,1)S(1)}, bf16[128,2048]{1,0:T(8,128)(2,1)S(1)}, u32[]{:S(2)}, u32[]{:S(2)}) collective-permute-start(bf16[128,2048]{1,0:T(8,128)(2,1)S(1)} %get-tuple-element.11), channel_id=1, source_target_pairs={{0,1},{1,0},{2,3},{3,2},{4,5},{5,4},{6,7},{7,6},{8,9},{9,8},{10,11... | collective-permute-start | bytes 1572872 | tf_op jit(solution)/shard_map/ppermute | solution.py:235
  174.8 8.8 %all-to-all-start.5 = ((f32[16,1,1]{2,1,0:T(1,128)}), f32[16,1,1]{2,1,0:T(1,128)S(1)}, u32[]{:S(2)}, u32[]{:S(2)}) async-start(f32[16,1,1]{2,1,0:T(1,128)} %broadcast_in_dim.65), calls=%async_computation.6 | async-start | bytes 16384 | tf_op jit(solution)/shard_map/all_to_all | solution.py:229
Sparse Core Ops, SparseCore 0:
  10.7 83.4 all-gather.1
  115.7 80.2 reduce-scatter.1
